TPU v7x, 128 devices: a whole 4x4x4 slice. The times are simulated.
128 devices in a mesh: gx: 8 (over y, x_hi), gy: 8 (over x_lo, z), mem: 2 (over core).
Axes of the slice: x: 4 (x_hi: 2, x_lo: 2; x = x_hi * 2 + x_lo), y: 4, z: 4, core: 2. Of those that a mesh axis runs over, the one named last changes fastest.
Arguments:
- src_hist: bfloat16 [4, 256, 1024, 128], P('mem', 'gx', 'gy'), may hold values from -6 to 6
- rec_p: float32 [256, 1024, 128], P('gx', 'gy'), may hold values from -6 to 6
- rec_q: float32 [256, 1024, 128], P('gx', 'gy'), may hold values from -6 to 6
- prev_p: float32 [256, 1024, 128], P('gx', 'gy'), may hold values from -6 to 6
- prev_q: float32 [256, 1024, 128], P('gx', 'gy'), may hold values from -6 to 6
- horiz: float32 [256, 1024, 128], P('gx', 'gy'), may hold values from 0.04 to 0.12
- vert: float32 [256, 1024, 128], P('gx', 'gy'), may hold values from 0.04 to 0.12
- ratio: float32 [256, 1024, 128], P('gx', 'gy'), may hold values from 0.6 to 1
- tilt: float32 [256, 1024, 128], P('gx', 'gy'), may hold values from -0.4 to 0.4
- rec_pos: int32 [4096], replicated, may hold values from 0 to 33554431
- rec_data: float32 [4, 4096], replicated, may hold values from -6 to 6
- lag_offs: int32 [2, 2], P('mem'), may hold values from -8 to 8, as said below
Outputs:
- image: float32 [2, 256, 1024, 128], P('mem', 'gx', 'gy')
- out_p: float32 [256, 1024, 128], P('gx', 'gy')
- out_q: float32 [256, 1024, 128], P('gx', 'gy')
Inputs may be any that keep to these rules, and one draw needn't show every extreme that they name: `lag_offs`: each offset lies within -8 .. 8; the offset pair (8, -8) occurs in every draw.
All inputs are finite; a program needn't handle non-finite values.
Results may differ from a plain program's by a relative error of at most 0.0003.
Values may be sent and summed in bfloat16 or wider, within the bound.
A program may use at most 128 MiB of HBM per device.

v0:
```python
import jax
import jax.numpy as jnp
from jax import lax
from jax.sharding import PartitionSpec as P

NT = 4
HMAX = 8


def with_halo(cells, sides, width):
    for axis, dim in sides:
        count = lax.axis_size(axis)
        ends = count - 1
        head = lax.slice_in_dim(cells, 0, width, axis=dim)
        tail = lax.slice_in_dim(cells, cells.shape[dim] - width, cells.shape[dim], axis=dim)
        cells = jnp.concatenate(
            [
                lax.ppermute(tail, axis, [(i, (i + 1) % count) for i in range(ends)]),
                cells,
                lax.ppermute(head, axis, [((i + 1) % count, i) for i in range(ends)]),
            ],
            axis=dim,
        )
    return cells


def advance(p, q, old_p, old_q, wide_p, wide_q, horiz, vert, ratio, tilt):
    lateral = wide_p[2:, 1:-1] + wide_p[:-2, 1:-1] + wide_p[1:-1, 2:] + wide_p[1:-1, :-2] - 4.0 * p
    deep = jnp.pad(wide_q[:, 1:-1], ((0, 0), (0, 0), (1, 1)))
    center = deep[1:-1]
    second = center[:, :, 2:] + center[:, :, :-2] - 2.0 * q
    mixed = 0.25 * (deep[2:, :, 2:] - deep[2:, :, :-2] - deep[:-2, :, 2:] + deep[:-2, :, :-2])
    horizontal = horiz * lateral
    upright = vert * (second + tilt * mixed)
    new_p = 2.0 * p - old_p + horizontal + upright
    new_q = 2.0 * q - old_q + ratio * horizontal + upright
    return (new_p, new_q)


def body(
    src_hist, rec_p, rec_q, prev_p, prev_q, horiz, vert, ratio, tilt, rec_pos, rec_data, lag_offs
):
    shape = rec_p.shape
    width_x, width_y, depth = shape
    cells = width_x * width_y * depth
    start_x = lax.axis_index("gx") * width_x
    start_y = lax.axis_index("gy") * width_y
    plane = width_y * lax.axis_size("gy") * depth
    glob_x = rec_pos // plane
    rest = rec_pos % plane
    glob_y = rest // depth
    glob_z = rest % depth
    local_x = glob_x - start_x
    local_y = glob_y - start_y
    inside = (local_x >= 0) & (local_x < width_x) & (local_y >= 0) & (local_y < width_y)
    target = jnp.where(inside, local_x * (width_y * depth) + local_y * depth + glob_z, cells)
    history = lax.all_gather(src_hist, "mem", axis=0, tiled=True)

    def snapshot_at(t):
        snap = lax.dynamic_index_in_dim(history, t, 0, keepdims=False)
        return with_halo(snap, (("gx", 0), ("gy", 1)), HMAX)

    fields = jnp.stack([rec_p, rec_q])
    older = jnp.stack([prev_p, prev_q])
    image = jnp.zeros((lag_offs.shape[0],) + shape, jnp.float32)

    def advance_step(k, carry):
        fields, older, image = carry
        t = NT - 1 - k
        wide_s = snapshot_at(t)
        current = fields[0]

        def one_lag(offset):
            piece = lax.dynamic_slice(
                wide_s, (HMAX - offset[0], HMAX - offset[1], jnp.int32(0)), shape
            )
            return piece.astype(jnp.float32) * current

        image = image + jax.vmap(one_lag)(lag_offs)
        wide = with_halo(fields, (("gx", 1), ("gy", 2)), 1)
        new_p, new_q = advance(
            fields[0], fields[1], older[0], older[1], wide[0], wide[1], horiz, vert, ratio, tilt
        )
        amount = lax.dynamic_index_in_dim(rec_data, t, 0, keepdims=False)
        new_p = new_p.reshape(-1).at[target].add(amount, mode="drop").reshape(shape)
        new_q = new_q.reshape(-1).at[target].add(amount, mode="drop").reshape(shape)
        return (jnp.stack([new_p, new_q]), fields, image)

    fields, older, image = lax.fori_loop(0, NT, advance_step, (fields, older, image))
    return (image, fields[0], fields[1])


def solution(mesh):
    placed = (
        P("mem", "gx", "gy", None),
        P("gx", "gy", None),
        P("gx", "gy", None),
        P("gx", "gy", None),
        P("gx", "gy", None),
        P("gx", "gy", None),
        P("gx", "gy", None),
        P("gx", "gy", None),
        P("gx", "gy", None),
        P(),
        P(),
        P("mem", None),
    )
    return jax.shard_map(
        body,
        mesh=mesh,
        in_specs=placed,
        out_specs=(P("mem", "gx", "gy", None), P("gx", "gy", None), P("gx", "gy", None)),
        check_vma=False,
    )
```

profile of v0, /device:TPU:6, one launch (start us, length us, event | category | flops | bytes accessed | tf_op | source)
XLA Modules:
  0.0 521.3 jit_solution(17456568272847188169)
XLA Ops:
  11.3 7.1 %pad_maximum_fusion.5 = (f32[2,32,128,128]{3,2,1,0:T(8,128)}, f32[2,32,128,128]{3,2,1,0:T(8,128)}) fusion(f32[1,32,128,128]{3,2,1,0:T(8,128)S(1)} %bitcast.95, f32[1,32,128,128]{3,2,1,0:T(8,128)} %bitcast.96, f32[1,32,128,128]{3,2,1,0:T(8,128)} %bitcast.97, f32[1,32,128,128]{3,2,1,0:T(8,128)} %bitcast.98), kind=kLoop, calls=%fused_computation.55 | loop fusion | flops 2097152 | bytes 16777216 | tf_op jit(solution)/shard_map/stack | solution.py:63
  18.4 10.1 %all-gather.2.cloned.1.call-done = bf16[4,32,128,128]{3,2,1,0:T(8,128)(2,1)} async-done(((bf16[2,32,128,128]{3,2,1,0:T(8,128)(2,1)}), bf16[4,32,128,128]{3,2,1,0:T(8,128)(2,1)}) %all-gather.2.cloned.1.call-update) | async-done | bytes 4194320 | tf_op jit(solution)/shard_map/all_gather | solution.py:57
  28.5 481.3 %while.21 = (s32[]{:T(128)}, f32[2,32,128,128]{3,2,1,0:T(8,128)}, f32[2,32,128,128]{3,2,1,0:T(8,128)}, f32[1,32,128,128]{3,2,1,0:T(8,128)}, f32[32,128,128]{2,1,...) while((s32[]{:T(128)}, f32[2,32,128,128]{3,2,1,0:T(8,128)}, ...), condition=%wide.region_3.4_spmd.clone, body=%wide.region_0.3_spmd.clone.sunk | while | flops 24369160 | bytes 151364336 | solution.py:89
  29.5 4.3 collective-permute-start
  33.8 3.1 collective-permute-start.1
  40.6 6.3 %collective-permute-start.5 = (bf16[8,128,128]{2,1,0:T(8,128)(2,1)}, bf16[8,128,128]{2,1,0:T(8,128)(2,1)}, u32[]{:S(2)}, u32[]{:S(2)}) collective-permute-start(bf16[8,128,128]{2,1,0:T(8,128)(2,1)} %get-tuple-element.500), channel_id=1, source_target_pairs={{0,16},{16,32},{32,48},{48,64},{64,80},{80,96},{96,112},{1,17},{17... | collective-permute-start | bytes 786440 | tf_op jit(solution)/shard_map/while/body/eval_jaxpr/ppermute | solution.py:18
  49.2 2.5 constant_dynamic-update-slice_fusion.7
  51.7 2.0 copy-done.2
  53.8 5.1 collective-permute-start.2
  61.5 5.4 %collective-permute-done.3 = f32[2,34,1,128]{3,2,1,0:T(1,128)S(1)} collective-permute-done((f32[2,34,1,128]{3,2,1,0:T(1,128)S(1)}, f32[2,34,1,128]{3,2,1,0:T(1,128)S(1)}, u32[]{:S(2)}, u32[]{:S(2)}) %collective-permute-start.3) | collective-permute-done | bytes 34848 | tf_op jit(solution)/shard_map/while/body/eval_jaxpr/ppermute | solution.py:18
  66.9 2.7 pad_maximum_fusion.10
  72.1 7.0 %fusion.40 = (f32[32,128,128]{2,1,0:T(8,128)S(1)}, f32[32,128,128]{2,1,0:T(8,128)S(1)}, f32[32,128,128]{2,1,0:T(8,128)}) fusion(f32[2,32,128,128]{3,2,1,0:T(8,128)} %get-tuple-element.522, f32[2,32,128,128]{3,2,1,0:T(8,128)S(1)} %copy-done.1, f32[32,128,128]{2,1,0:T(8,128)} %get-tuple-element.541, f32[34,130,128]{2,1,0:T(8,128)S(1)} %get-tuple-element.492, ...), kind=kLoop, calls=%fused_computation.32.clone.1 | loop fusion | flops 10485760 | bytes 29491200 | tf_op jit(solution)/shard_map/while/body/eval_jaxpr/add | solution.py:35
  82.5 6.0 %collective-permute-start.7 = (bf16[48,8,128]{2,1,0:T(8,128)(2,1)}, bf16[48,8,128]{2,1,0:T(8,128)(2,1)}, u32[]{:S(2)}, u32[]{:S(2)}) collective-permute-start(bf16[48,8,128]{2,1,0:T(8,128)(2,1)} %get-tuple-element.502), channel_id=1, source_target_pairs={{2,0},{4,2},{6,4},{8,6},{10,8},{12,10},{14,12},{3,1},{5,3},{7,5},{... | collective-permute-start | bytes 294920 | tf_op jit(solution)/shard_map/while/body/eval_jaxpr/ppermute | solution.py:20
  88.5 5.3 %fusion.41 = f32[32,128,128]{2,1,0:T(8,128)} fusion(f32[32,128,128]{2,1,0:T(8,128)} %get-tuple-element.494, f32[32,128,128]{2,1,0:T(8,128)} %get-tuple-element.546, f32[32,128,128]{2,1,0:T(8,128)S(1)} %get-tuple-element.495, f32[2,32,128,128]{3,2,1,0:T(8,128)} %get-tuple-element.522, f32[2,32,128,128]{3,2,1,0:T(8,128)S(1)} %copy-done.1), kind=kLoop, calls=%fused_computation.30.clone.1 | loop fusion | flops 2621440 | bytes 12582912 | tf_op jit(solution)/shard_map/while/body/eval_jaxpr/add | solution.py:36
  95.8 22.9 %scatter_fusion = f32[524288]{0:T(1024)} fusion(f32[524288]{0:T(1024)} %bitcast.89, s32[4096]{0:T(1024)S(1)} %bitcast.93, f32[4096]{0:T(1024)S(1)} %bitcast.91), kind=kCustom, calls=%fused_computation.1.clone.clone.1 | custom fusion | flops 4096 | bytes 65536 | tf_op jit(solution)/shard_map/while/body/eval_jaxpr/scatter-add | solution.py:86
  118.7 23.2 %scatter_fusion.1 = f32[524288]{0:T(1024)S(1)} fusion(f32[524288]{0:T(1024)S(1)} %bitcast.87, s32[4096]{0:T(1024)S(1)} %bitcast.94, f32[4096]{0:T(1024)S(1)} %bitcast.92), kind=kCustom, calls=%fused_computation.clone.clone.1 | custom fusion | flops 4096 | bytes 65536 | tf_op jit(solution)/shard_map/while/body/eval_jaxpr/scatter-add | solution.py:85
  141.9 6.5 %fusion.43 = f32[1,32,128,128]{3,2,1,0:T(8,128)} fusion(f32[1,32,128,128]{3,2,1,0:T(8,128)} %get-tuple-element.523, f32[2,32,128,128]{3,2,1,0:T(8,128)} %get-tuple-element.521, s32[]{:T(128)} %bitcast.85, s32[]{:T(128)} %bitcast.86, bf16[48,8,128]{2,1,0:T(8,128)(2,1)S(1)} %collective-permute-done.6, bf16[8,128,128]{2,1,0:T(8,128)(2,1)} %collective-permute-done.5, ...), kind=kLoop, calls=%fused_computation.27.clone.1 | loop fusion | flops 7340032 | bytes 8060937 | tf_op jit(solution)/shard_map/while/body/eval_jaxpr/add | solution.py:79
  148.4 2.3 pad_maximum_fusion.11
  151.7 4.0 collective-permute-start
  155.7 3.4 collective-permute-start.1
  162.9 6.3 %collective-permute-start.5 = (bf16[8,128,128]{2,1,0:T(8,128)(2,1)}, bf16[8,128,128]{2,1,0:T(8,128)(2,1)}, u32[]{:S(2)}, u32[]{:S(2)}) collective-permute-start(bf16[8,128,128]{2,1,0:T(8,128)(2,1)} %get-tuple-element.500), channel_id=1, source_target_pairs={{0,16},{16,32},{32,48},{48,64},{64,80},{80,96},{96,112},{1,17},{17... | collective-permute-start | bytes 786440 | tf_op jit(solution)/shard_map/while/body/eval_jaxpr/ppermute | solution.py:18
  171.5 2.5 constant_dynamic-update-slice_fusion.7
  174.0 2.0 copy-done.2
  178.0 3.9 collective-permute-start.3
  182.5 3.4 collective-permute-done.3
  185.9 2.7 pad_maximum_fusion.10
  191.2 7.0 %fusion.40 = (f32[32,128,128]{2,1,0:T(8,128)S(1)}, f32[32,128,128]{2,1,0:T(8,128)S(1)}, f32[32,128,128]{2,1,0:T(8,128)}) fusion(f32[2,32,128,128]{3,2,1,0:T(8,128)} %get-tuple-element.522, f32[2,32,128,128]{3,2,1,0:T(8,128)S(1)} %copy-done.1, f32[32,128,128]{2,1,0:T(8,128)} %get-tuple-element.541, f32[34,130,128]{2,1,0:T(8,128)S(1)} %get-tuple-element.492, ...), kind=kLoop, calls=%fused_computation.32.clone.1 | loop fusion | flops 10485760 | bytes 29491200 | tf_op jit(solution)/shard_map/while/body/eval_jaxpr/add | solution.py:35
  201.6 6.0 %collective-permute-start.7 = (bf16[48,8,128]{2,1,0:T(8,128)(2,1)}, bf16[48,8,128]{2,1,0:T(8,128)(2,1)}, u32[]{:S(2)}, u32[]{:S(2)}) collective-permute-start(bf16[48,8,128]{2,1,0:T(8,128)(2,1)} %get-tuple-element.502), channel_id=1, source_target_pairs={{2,0},{4,2},{6,4},{8,6},{10,8},{12,10},{14,12},{3,1},{5,3},{7,5},{... | collective-permute-start | bytes 294920 | tf_op jit(solution)/shard_map/while/body/eval_jaxpr/ppermute | solution.py:20
  207.6 5.3 %fusion.41 = f32[32,128,128]{2,1,0:T(8,128)} fusion(f32[32,128,128]{2,1,0:T(8,128)} %get-tuple-element.494, f32[32,128,128]{2,1,0:T(8,128)} %get-tuple-element.546, f32[32,128,128]{2,1,0:T(8,128)S(1)} %get-tuple-element.495, f32[2,32,128,128]{3,2,1,0:T(8,128)} %get-tuple-element.522, f32[2,32,128,128]{3,2,1,0:T(8,128)S(1)} %copy-done.1), kind=kLoop, calls=%fused_computation.30.clone.1 | loop fusion | flops 2621440 | bytes 12582912 | tf_op jit(solution)/shard_map/while/body/eval_jaxpr/add | solution.py:36
  214.9 22.9 %scatter_fusion = f32[524288]{0:T(1024)} fusion(f32[524288]{0:T(1024)} %bitcast.89, s32[4096]{0:T(1024)S(1)} %bitcast.93, f32[4096]{0:T(1024)S(1)} %bitcast.91), kind=kCustom, calls=%fused_computation.1.clone.clone.1 | custom fusion | flops 4096 | bytes 65536 | tf_op jit(solution)/shard_map/while/body/eval_jaxpr/scatter-add | solution.py:86
  237.8 23.2 %scatter_fusion.1 = f32[524288]{0:T(1024)S(1)} fusion(f32[524288]{0:T(1024)S(1)} %bitcast.87, s32[4096]{0:T(1024)S(1)} %bitcast.94, f32[4096]{0:T(1024)S(1)} %bitcast.92), kind=kCustom, calls=%fused_computation.clone.clone.1 | custom fusion | flops 4096 | bytes 65536 | tf_op jit(solution)/shard_map/while/body/eval_jaxpr/scatter-add | solution.py:85
  261.0 7.1 %fusion.43 = f32[1,32,128,128]{3,2,1,0:T(8,128)} fusion(f32[1,32,128,128]{3,2,1,0:T(8,128)} %get-tuple-element.523, f32[2,32,128,128]{3,2,1,0:T(8,128)} %get-tuple-element.521, s32[]{:T(128)} %bitcast.85, s32[]{:T(128)} %bitcast.86, bf16[48,8,128]{2,1,0:T(8,128)(2,1)S(1)} %collective-permute-done.6, bf16[8,128,128]{2,1,0:T(8,128)(2,1)} %collective-permute-done.5, ...), kind=kLoop, calls=%fused_computation.27.clone.1 | loop fusion | flops 7340032 | bytes 8060937 | tf_op jit(solution)/shard_map/while/body/eval_jaxpr/add | solution.py:79
  268.1 2.3 pad_maximum_fusion.11
  271.4 4.0 collective-permute-start
  275.4 3.4 collective-permute-start.1
  282.6 6.3 %collective-permute-start.5 = (bf16[8,128,128]{2,1,0:T(8,128)(2,1)}, bf16[8,128,128]{2,1,0:T(8,128)(2,1)}, u32[]{:S(2)}, u32[]{:S(2)}) collective-permute-start(bf16[8,128,128]{2,1,0:T(8,128)(2,1)} %get-tuple-element.500), channel_id=1, source_target_pairs={{0,16},{16,32},{32,48},{48,64},{64,80},{80,96},{96,112},{1,17},{17... | collective-permute-start | bytes 786440 | tf_op jit(solution)/shard_map/while/body/eval_jaxpr/ppermute | solution.py:18
  291.1 2.5 constant_dynamic-update-slice_fusion.7
  293.6 2.0 copy-done.2
  297.7 3.9 collective-permute-start.3
  302.2 3.4 collective-permute-done.3
  305.6 2.7 pad_maximum_fusion.10
  310.9 7.0 %fusion.40 = (f32[32,128,128]{2,1,0:T(8,128)S(1)}, f32[32,128,128]{2,1,0:T(8,128)S(1)}, f32[32,128,128]{2,1,0:T(8,128)}) fusion(f32[2,32,128,128]{3,2,1,0:T(8,128)} %get-tuple-element.522, f32[2,32,128,128]{3,2,1,0:T(8,128)S(1)} %copy-done.1, f32[32,128,128]{2,1,0:T(8,128)} %get-tuple-element.541, f32[34,130,128]{2,1,0:T(8,128)S(1)} %get-tuple-element.492, ...), kind=kLoop, calls=%fused_computation.32.clone.1 | loop fusion | flops 10485760 | bytes 29491200 | tf_op jit(solution)/shard_map/while/body/eval_jaxpr/add | solution.py:35
  321.2 6.0 %collective-permute-start.7 = (bf16[48,8,128]{2,1,0:T(8,128)(2,1)}, bf16[48,8,128]{2,1,0:T(8,128)(2,1)}, u32[]{:S(2)}, u32[]{:S(2)}) collective-permute-start(bf16[48,8,128]{2,1,0:T(8,128)(2,1)} %get-tuple-element.502), channel_id=1, source_target_pairs={{2,0},{4,2},{6,4},{8,6},{10,8},{12,10},{14,12},{3,1},{5,3},{7,5},{... | collective-permute-start | bytes 294920 | tf_op jit(solution)/shard_map/while/body/eval_jaxpr/ppermute | solution.py:20
  327.3 5.3 %fusion.41 = f32[32,128,128]{2,1,0:T(8,128)} fusion(f32[32,128,128]{2,1,0:T(8,128)} %get-tuple-element.494, f32[32,128,128]{2,1,0:T(8,128)} %get-tuple-element.546, f32[32,128,128]{2,1,0:T(8,128)S(1)} %get-tuple-element.495, f32[2,32,128,128]{3,2,1,0:T(8,128)} %get-tuple-element.522, f32[2,32,128,128]{3,2,1,0:T(8,128)S(1)} %copy-done.1), kind=kLoop, calls=%fused_computation.30.clone.1 | loop fusion | flops 2621440 | bytes 12582912 | tf_op jit(solution)/shard_map/while/body/eval_jaxpr/add | solution.py:36
  334.5 22.9 %scatter_fusion = f32[524288]{0:T(1024)} fusion(f32[524288]{0:T(1024)} %bitcast.89, s32[4096]{0:T(1024)S(1)} %bitcast.93, f32[4096]{0:T(1024)S(1)} %bitcast.91), kind=kCustom, calls=%fused_computation.1.clone.clone.1 | custom fusion | flops 4096 | bytes 65536 | tf_op jit(solution)/shard_map/while/body/eval_jaxpr/scatter-add | solution.py:86
  357.4 23.2 %scatter_fusion.1 = f32[524288]{0:T(1024)S(1)} fusion(f32[524288]{0:T(1024)S(1)} %bitcast.87, s32[4096]{0:T(1024)S(1)} %bitcast.94, f32[4096]{0:T(1024)S(1)} %bitcast.92), kind=kCustom, calls=%fused_computation.clone.clone.1 | custom fusion | flops 4096 | bytes 65536 | tf_op jit(solution)/shard_map/while/body/eval_jaxpr/scatter-add | solution.py:85
  380.7 7.1 %fusion.43 = f32[1,32,128,128]{3,2,1,0:T(8,128)} fusion(f32[1,32,128,128]{3,2,1,0:T(8,128)} %get-tuple-element.523, f32[2,32,128,128]{3,2,1,0:T(8,128)} %get-tuple-element.521, s32[]{:T(128)} %bitcast.85, s32[]{:T(128)} %bitcast.86, bf16[48,8,128]{2,1,0:T(8,128)(2,1)S(1)} %collective-permute-done.6, bf16[8,128,128]{2,1,0:T(8,128)(2,1)} %collective-permute-done.5, ...), kind=kLoop, calls=%fused_computation.27.clone.1 | loop fusion | flops 7340032 | bytes 8060937 | tf_op jit(solution)/shard_map/while/body/eval_jaxpr/add | solution.py:79
  387.8 2.3 pad_maximum_fusion.11
  391.1 4.0 collective-permute-start
  395.1 3.4 collective-permute-start.1
  402.2 6.3 %collective-permute-start.5 = (bf16[8,128,128]{2,1,0:T(8,128)(2,1)}, bf16[8,128,128]{2,1,0:T(8,128)(2,1)}, u32[]{:S(2)}, u32[]{:S(2)}) collective-permute-start(bf16[8,128,128]{2,1,0:T(8,128)(2,1)} %get-tuple-element.500), channel_id=1, source_target_pairs={{0,16},{16,32},{32,48},{48,64},{64,80},{80,96},{96,112},{1,17},{17... | collective-permute-start | bytes 786440 | tf_op jit(solution)/shard_map/while/body/eval_jaxpr/ppermute | solution.py:18
  410.8 2.5 constant_dynamic-update-slice_fusion.7
  413.3 2.0 copy-done.2
  417.3 3.9 collective-permute-start.3
  421.9 3.4 collective-permute-done.3
  425.3 2.7 pad_maximum_fusion.10
  430.5 7.0 %fusion.40 = (f32[32,128,128]{2,1,0:T(8,128)S(1)}, f32[32,128,128]{2,1,0:T(8,128)S(1)}, f32[32,128,128]{2,1,0:T(8,128)}) fusion(f32[2,32,128,128]{3,2,1,0:T(8,128)} %get-tuple-element.522, f32[2,32,128,128]{3,2,1,0:T(8,128)S(1)} %copy-done.1, f32[32,128,128]{2,1,0:T(8,128)} %get-tuple-element.541, f32[34,130,128]{2,1,0:T(8,128)S(1)} %get-tuple-element.492, ...), kind=kLoop, calls=%fused_computation.32.clone.1 | loop fusion | flops 10485760 | bytes 29491200 | tf_op jit(solution)/shard_map/while/body/eval_jaxpr/add | solution.py:35
  440.9 6.0 %collective-permute-start.7 = (bf16[48,8,128]{2,1,0:T(8,128)(2,1)}, bf16[48,8,128]{2,1,0:T(8,128)(2,1)}, u32[]{:S(2)}, u32[]{:S(2)}) collective-permute-start(bf16[48,8,128]{2,1,0:T(8,128)(2,1)} %get-tuple-element.502), channel_id=1, source_target_pairs={{2,0},{4,2},{6,4},{8,6},{10,8},{12,10},{14,12},{3,1},{5,3},{7,5},{... | collective-permute-start | bytes 294920 | tf_op jit(solution)/shard_map/while/body/eval_jaxpr/ppermute | solution.py:20
  446.9 5.3 %fusion.41 = f32[32,128,128]{2,1,0:T(8,128)} fusion(f32[32,128,128]{2,1,0:T(8,128)} %get-tuple-element.494, f32[32,128,128]{2,1,0:T(8,128)} %get-tuple-element.546, f32[32,128,128]{2,1,0:T(8,128)S(1)} %get-tuple-element.495, f32[2,32,128,128]{3,2,1,0:T(8,128)} %get-tuple-element.522, f32[2,32,128,128]{3,2,1,0:T(8,128)S(1)} %copy-done.1), kind=kLoop, calls=%fused_computation.30.clone.1 | loop fusion | flops 2621440 | bytes 12582912 | tf_op jit(solution)/shard_map/while/body/eval_jaxpr/add | solution.py:36
  454.2 22.9 %scatter_fusion = f32[524288]{0:T(1024)} fusion(f32[524288]{0:T(1024)} %bitcast.89, s32[4096]{0:T(1024)S(1)} %bitcast.93, f32[4096]{0:T(1024)S(1)} %bitcast.91), kind=kCustom, calls=%fused_computation.1.clone.clone.1 | custom fusion | flops 4096 | bytes 65536 | tf_op jit(solution)/shard_map/while/body/eval_jaxpr/scatter-add | solution.py:86
  477.1 23.2 %scatter_fusion.1 = f32[524288]{0:T(1024)S(1)} fusion(f32[524288]{0:T(1024)S(1)} %bitcast.87, s32[4096]{0:T(1024)S(1)} %bitcast.94, f32[4096]{0:T(1024)S(1)} %bitcast.92), kind=kCustom, calls=%fused_computation.clone.clone.1 | custom fusion | flops 4096 | bytes 65536 | tf_op jit(solution)/shard_map/while/body/eval_jaxpr/scatter-add | solution.py:85
  500.3 7.1 %fusion.43 = f32[1,32,128,128]{3,2,1,0:T(8,128)} fusion(f32[1,32,128,128]{3,2,1,0:T(8,128)} %get-tuple-element.523, f32[2,32,128,128]{3,2,1,0:T(8,128)} %get-tuple-element.521, s32[]{:T(128)} %bitcast.85, s32[]{:T(128)} %bitcast.86, bf16[48,8,128]{2,1,0:T(8,128)(2,1)S(1)} %collective-permute-done.6, bf16[8,128,128]{2,1,0:T(8,128)(2,1)} %collective-permute-done.5, ...), kind=kLoop, calls=%fused_computation.27.clone.1 | loop fusion | flops 7340032 | bytes 8060937 | tf_op jit(solution)/shard_map/while/body/eval_jaxpr/add | solution.py:79
  507.5 2.3 pad_maximum_fusion.11
  509.8 4.7 slice_bitcast_fusion.2
  (140 shorter events, 70.8 us)
Async XLA Ops:
  7.2 0.8 copy-start.7
  7.2 4.0 copy-start.6
  7.2 4.1 copy-start.3
  7.2 21.3 %all-gather.2.cloned.1.call-start = ((), (), s32[]{:S(2)}) async-start(), calls=%async_computation | async-start | bytes 6291456 | tf_op jit(solution)/shard_map/all_gather | solution.py:57
  28.5 32.4 %copy-start.4 = (s32[1,3]{1,0:T(1,128)}, s32[1,3]{1,0:T(1,128)S(1)}, u32[]{:S(2)}) copy-start(s32[1,3]{1,0:T(1,128)S(1)} %get-tuple-element.548) | copy-start | bytes 40 | tf_op jit(solution)/shard_map/while
  29.5 19.7 %collective-permute-start = (f32[2,1,128,128]{3,2,1,0:T(8,128)S(1)}, f32[2,1,128,128]{3,2,1,0:T(8,128)S(1)}, u32[]{:S(2)}, u32[]{:S(2)}) collective-permute-start(f32[2,1,128,128]{3,2,1,0:T(8,128)S(1)} %get-tuple-element.488), channel_id=1, source_target_pairs={{0,16},{16,32},{32,48},{48,64},{64,80},{80,96},{96,112},{1,17},{17... | collective-permute-start | bytes 393224 | tf_op jit(solution)/shard_map/while/body/eval_jaxpr/ppermute | solution.py:18
  33.8 17.9 %collective-permute-start.1 = (f32[2,1,128,128]{3,2,1,0:T(8,128)S(1)}, f32[2,1,128,128]{3,2,1,0:T(8,128)S(1)}, u32[]{:S(2)}, u32[]{:S(2)}) collective-permute-start(f32[2,1,128,128]{3,2,1,0:T(8,128)S(1)} %get-tuple-element.489), channel_id=1, source_target_pairs={{16,0},{32,16},{48,32},{64,48},{80,64},{96,80},{112,96},{17,1},{33... | collective-permute-start | bytes 393224 | tf_op jit(solution)/shard_map/while/body/eval_jaxpr/ppermute | solution.py:20
  38.7 40.4 %collective-permute-start.4 = (bf16[8,128,128]{2,1,0:T(8,128)(2,1)}, bf16[8,128,128]{2,1,0:T(8,128)(2,1)S(1)}, u32[]{:S(2)}, u32[]{:S(2)}) collective-permute-start(bf16[8,128,128]{2,1,0:T(8,128)(2,1)} %get-tuple-element.499), channel_id=1, source_target_pairs={{16,0},{32,16},{48,32},{64,48},{80,64},{96,80},{112,96},{17,1},{33... | collective-permute-start | bytes 786440 | tf_op jit(solution)/shard_map/while/body/eval_jaxpr/ppermute | solution.py:20
  40.6 38.5 %collective-permute-start.5 = (bf16[8,128,128]{2,1,0:T(8,128)(2,1)}, bf16[8,128,128]{2,1,0:T(8,128)(2,1)}, u32[]{:S(2)}, u32[]{:S(2)}) collective-permute-start(bf16[8,128,128]{2,1,0:T(8,128)(2,1)} %get-tuple-element.500), channel_id=1, source_target_pairs={{0,16},{16,32},{32,48},{48,64},{64,80},{80,96},{96,112},{1,17},{17... | collective-permute-start | bytes 786440 | tf_op jit(solution)/shard_map/while/body/eval_jaxpr/ppermute | solution.py:18
  51.7 2.1 copy-start.2
  53.8 7.7 %collective-permute-start.2 = (f32[2,34,1,128]{3,2,1,0:T(1,128)S(1)}, f32[2,34,1,128]{3,2,1,0:T(1,128)S(1)}, u32[]{:S(2)}, u32[]{:S(2)}) collective-permute-start(f32[2,34,1,128]{3,2,1,0:T(1,128)S(1)} %get-tuple-element.490), channel_id=1, source_target_pairs={{2,0},{4,2},{6,4},{8,6},{10,8},{12,10},{14,12},{3,1},{5,3},{7,5},{... | collective-permute-start | bytes 104456 | tf_op jit(solution)/shard_map/while/body/eval_jaxpr/ppermute | solution.py:20
  59.0 7.9 %collective-permute-start.3 = (f32[2,34,1,128]{3,2,1,0:T(1,128)S(1)}, f32[2,34,1,128]{3,2,1,0:T(1,128)S(1)}, u32[]{:S(2)}, u32[]{:S(2)}) collective-permute-start(f32[2,34,1,128]{3,2,1,0:T(1,128)S(1)} %get-tuple-element.491), channel_id=1, source_target_pairs={{0,2},{2,4},{4,6},{6,8},{8,10},{10,12},{12,14},{1,3},{3,5},{5,7},{... | collective-permute-start | bytes 104456 | tf_op jit(solution)/shard_map/while/body/eval_jaxpr/ppermute | solution.py:18
  70.0 2.2 copy-start.1
  80.6 61.3 %collective-permute-start.6 = (bf16[48,8,128]{2,1,0:T(8,128)(2,1)}, bf16[48,8,128]{2,1,0:T(8,128)(2,1)S(1)}, u32[]{:S(2)}, u32[]{:S(2)}) collective-permute-start(bf16[48,8,128]{2,1,0:T(8,128)(2,1)} %get-tuple-element.501), channel_id=1, source_target_pairs={{0,2},{2,4},{4,6},{6,8},{8,10},{10,12},{12,14},{1,3},{3,5},{5,7},{... | collective-permute-start | bytes 294920 | tf_op jit(solution)/shard_map/while/body/eval_jaxpr/ppermute | solution.py:18
  82.5 59.4 %collective-permute-start.7 = (bf16[48,8,128]{2,1,0:T(8,128)(2,1)}, bf16[48,8,128]{2,1,0:T(8,128)(2,1)}, u32[]{:S(2)}, u32[]{:S(2)}) collective-permute-start(bf16[48,8,128]{2,1,0:T(8,128)(2,1)} %get-tuple-element.502), channel_id=1, source_target_pairs={{2,0},{4,2},{6,4},{8,6},{10,8},{12,10},{14,12},{3,1},{5,3},{7,5},{... | collective-permute-start | bytes 294920 | tf_op jit(solution)/shard_map/while/body/eval_jaxpr/ppermute | solution.py:20
  141.9 6.5 %copy-start = (f32[524288]{0:T(1024)S(1)}, f32[524288]{0:T(1024)}, u32[]{:S(2)}) copy-start(f32[524288]{0:T(1024)} %scatter_fusion) | copy-start | bytes 6291460 | tf_op jit(solution)/shard_map/while
  148.4 2.3 copy-start.5
  150.7 31.2 %copy-start.4 = (s32[1,3]{1,0:T(1,128)}, s32[1,3]{1,0:T(1,128)S(1)}, u32[]{:S(2)}) copy-start(s32[1,3]{1,0:T(1,128)S(1)} %get-tuple-element.548) | copy-start | bytes 40 | tf_op jit(solution)/shard_map/while
  151.7 19.7 %collective-permute-start = (f32[2,1,128,128]{3,2,1,0:T(8,128)S(1)}, f32[2,1,128,128]{3,2,1,0:T(8,128)S(1)}, u32[]{:S(2)}, u32[]{:S(2)}) collective-permute-start(f32[2,1,128,128]{3,2,1,0:T(8,128)S(1)} %get-tuple-element.488), channel_id=1, source_target_pairs={{0,16},{16,32},{32,48},{48,64},{64,80},{80,96},{96,112},{1,17},{17... | collective-permute-start | bytes 393224 | tf_op jit(solution)/shard_map/while/body/eval_jaxpr/ppermute | solution.py:18
  155.7 18.2 %collective-permute-start.1 = (f32[2,1,128,128]{3,2,1,0:T(8,128)S(1)}, f32[2,1,128,128]{3,2,1,0:T(8,128)S(1)}, u32[]{:S(2)}, u32[]{:S(2)}) collective-permute-start(f32[2,1,128,128]{3,2,1,0:T(8,128)S(1)} %get-tuple-element.489), channel_id=1, source_target_pairs={{16,0},{32,16},{48,32},{64,48},{80,64},{96,80},{112,96},{17,1},{33... | collective-permute-start | bytes 393224 | tf_op jit(solution)/shard_map/while/body/eval_jaxpr/ppermute | solution.py:20
  161.0 37.2 %collective-permute-start.4 = (bf16[8,128,128]{2,1,0:T(8,128)(2,1)}, bf16[8,128,128]{2,1,0:T(8,128)(2,1)S(1)}, u32[]{:S(2)}, u32[]{:S(2)}) collective-permute-start(bf16[8,128,128]{2,1,0:T(8,128)(2,1)} %get-tuple-element.499), channel_id=1, source_target_pairs={{16,0},{32,16},{48,32},{64,48},{80,64},{96,80},{112,96},{17,1},{33... | collective-permute-start | bytes 786440 | tf_op jit(solution)/shard_map/while/body/eval_jaxpr/ppermute | solution.py:20
  162.9 35.3 %collective-permute-start.5 = (bf16[8,128,128]{2,1,0:T(8,128)(2,1)}, bf16[8,128,128]{2,1,0:T(8,128)(2,1)}, u32[]{:S(2)}, u32[]{:S(2)}) collective-permute-start(bf16[8,128,128]{2,1,0:T(8,128)(2,1)} %get-tuple-element.500), channel_id=1, source_target_pairs={{0,16},{16,32},{32,48},{48,64},{64,80},{80,96},{96,112},{1,17},{17... | collective-permute-start | bytes 786440 | tf_op jit(solution)/shard_map/while/body/eval_jaxpr/ppermute | solution.py:18
  174.0 2.1 copy-start.2
  176.1 6.5 %collective-permute-start.2 = (f32[2,34,1,128]{3,2,1,0:T(1,128)S(1)}, f32[2,34,1,128]{3,2,1,0:T(1,128)S(1)}, u32[]{:S(2)}, u32[]{:S(2)}) collective-permute-start(f32[2,34,1,128]{3,2,1,0:T(1,128)S(1)} %get-tuple-element.490), channel_id=1, source_target_pairs={{2,0},{4,2},{6,4},{8,6},{10,8},{12,10},{14,12},{3,1},{5,3},{7,5},{... | collective-permute-start | bytes 104456 | tf_op jit(solution)/shard_map/while/body/eval_jaxpr/ppermute | solution.py:20
  178.0 7.9 %collective-permute-start.3 = (f32[2,34,1,128]{3,2,1,0:T(1,128)S(1)}, f32[2,34,1,128]{3,2,1,0:T(1,128)S(1)}, u32[]{:S(2)}, u32[]{:S(2)}) collective-permute-start(f32[2,34,1,128]{3,2,1,0:T(1,128)S(1)} %get-tuple-element.491), channel_id=1, source_target_pairs={{0,2},{2,4},{4,6},{6,8},{8,10},{10,12},{12,14},{1,3},{3,5},{5,7},{... | collective-permute-start | bytes 104456 | tf_op jit(solution)/shard_map/while/body/eval_jaxpr/ppermute | solution.py:18
  189.0 2.2 copy-start.1
  199.6 61.3 %collective-permute-start.6 = (bf16[48,8,128]{2,1,0:T(8,128)(2,1)}, bf16[48,8,128]{2,1,0:T(8,128)(2,1)S(1)}, u32[]{:S(2)}, u32[]{:S(2)}) collective-permute-start(bf16[48,8,128]{2,1,0:T(8,128)(2,1)} %get-tuple-element.501), channel_id=1, source_target_pairs={{0,2},{2,4},{4,6},{6,8},{8,10},{10,12},{12,14},{1,3},{3,5},{5,7},{... | collective-permute-start | bytes 294920 | tf_op jit(solution)/shard_map/while/body/eval_jaxpr/ppermute | solution.py:18
  201.6 59.4 %collective-permute-start.7 = (bf16[48,8,128]{2,1,0:T(8,128)(2,1)}, bf16[48,8,128]{2,1,0:T(8,128)(2,1)}, u32[]{:S(2)}, u32[]{:S(2)}) collective-permute-start(bf16[48,8,128]{2,1,0:T(8,128)(2,1)} %get-tuple-element.502), channel_id=1, source_target_pairs={{2,0},{4,2},{6,4},{8,6},{10,8},{12,10},{14,12},{3,1},{5,3},{7,5},{... | collective-permute-start | bytes 294920 | tf_op jit(solution)/shard_map/while/body/eval_jaxpr/ppermute | solution.py:20
  261.0 7.1 %copy-start = (f32[524288]{0:T(1024)S(1)}, f32[524288]{0:T(1024)}, u32[]{:S(2)}) copy-start(f32[524288]{0:T(1024)} %scatter_fusion) | copy-start | bytes 6291460 | tf_op jit(solution)/shard_map/while
  268.1 2.3 copy-start.5
  270.4 31.2 %copy-start.4 = (s32[1,3]{1,0:T(1,128)}, s32[1,3]{1,0:T(1,128)S(1)}, u32[]{:S(2)}) copy-start(s32[1,3]{1,0:T(1,128)S(1)} %get-tuple-element.548) | copy-start | bytes 40 | tf_op jit(solution)/shard_map/while
  271.4 19.7 %collective-permute-start = (f32[2,1,128,128]{3,2,1,0:T(8,128)S(1)}, f32[2,1,128,128]{3,2,1,0:T(8,128)S(1)}, u32[]{:S(2)}, u32[]{:S(2)}) collective-permute-start(f32[2,1,128,128]{3,2,1,0:T(8,128)S(1)} %get-tuple-element.488), channel_id=1, source_target_pairs={{0,16},{16,32},{32,48},{48,64},{64,80},{80,96},{96,112},{1,17},{17... | collective-permute-start | bytes 393224 | tf_op jit(solution)/shard_map/while/body/eval_jaxpr/ppermute | solution.py:18
  275.4 18.2 %collective-permute-start.1 = (f32[2,1,128,128]{3,2,1,0:T(8,128)S(1)}, f32[2,1,128,128]{3,2,1,0:T(8,128)S(1)}, u32[]{:S(2)}, u32[]{:S(2)}) collective-permute-start(f32[2,1,128,128]{3,2,1,0:T(8,128)S(1)} %get-tuple-element.489), channel_id=1, source_target_pairs={{16,0},{32,16},{48,32},{64,48},{80,64},{96,80},{112,96},{17,1},{33... | collective-permute-start | bytes 393224 | tf_op jit(solution)/shard_map/while/body/eval_jaxpr/ppermute | solution.py:20
  280.7 37.2 %collective-permute-start.4 = (bf16[8,128,128]{2,1,0:T(8,128)(2,1)}, bf16[8,128,128]{2,1,0:T(8,128)(2,1)S(1)}, u32[]{:S(2)}, u32[]{:S(2)}) collective-permute-start(bf16[8,128,128]{2,1,0:T(8,128)(2,1)} %get-tuple-element.499), channel_id=1, source_target_pairs={{16,0},{32,16},{48,32},{64,48},{80,64},{96,80},{112,96},{17,1},{33... | collective-permute-start | bytes 786440 | tf_op jit(solution)/shard_map/while/body/eval_jaxpr/ppermute | solution.py:20
  282.6 35.3 %collective-permute-start.5 = (bf16[8,128,128]{2,1,0:T(8,128)(2,1)}, bf16[8,128,128]{2,1,0:T(8,128)(2,1)}, u32[]{:S(2)}, u32[]{:S(2)}) collective-permute-start(bf16[8,128,128]{2,1,0:T(8,128)(2,1)} %get-tuple-element.500), channel_id=1, source_target_pairs={{0,16},{16,32},{32,48},{48,64},{64,80},{80,96},{96,112},{1,17},{17... | collective-permute-start | bytes 786440 | tf_op jit(solution)/shard_map/while/body/eval_jaxpr/ppermute | solution.py:18
  293.6 2.1 copy-start.2
  295.7 6.5 %collective-permute-start.2 = (f32[2,34,1,128]{3,2,1,0:T(1,128)S(1)}, f32[2,34,1,128]{3,2,1,0:T(1,128)S(1)}, u32[]{:S(2)}, u32[]{:S(2)}) collective-permute-start(f32[2,34,1,128]{3,2,1,0:T(1,128)S(1)} %get-tuple-element.490), channel_id=1, source_target_pairs={{2,0},{4,2},{6,4},{8,6},{10,8},{12,10},{14,12},{3,1},{5,3},{7,5},{... | collective-permute-start | bytes 104456 | tf_op jit(solution)/shard_map/while/body/eval_jaxpr/ppermute | solution.py:20
  297.7 7.9 %collective-permute-start.3 = (f32[2,34,1,128]{3,2,1,0:T(1,128)S(1)}, f32[2,34,1,128]{3,2,1,0:T(1,128)S(1)}, u32[]{:S(2)}, u32[]{:S(2)}) collective-permute-start(f32[2,34,1,128]{3,2,1,0:T(1,128)S(1)} %get-tuple-element.491), channel_id=1, source_target_pairs={{0,2},{2,4},{4,6},{6,8},{8,10},{10,12},{12,14},{1,3},{3,5},{5,7},{... | collective-permute-start | bytes 104456 | tf_op jit(solution)/shard_map/while/body/eval_jaxpr/ppermute | solution.py:18
  308.7 2.2 copy-start.1
  319.3 61.3 %collective-permute-start.6 = (bf16[48,8,128]{2,1,0:T(8,128)(2,1)}, bf16[48,8,128]{2,1,0:T(8,128)(2,1)S(1)}, u32[]{:S(2)}, u32[]{:S(2)}) collective-permute-start(bf16[48,8,128]{2,1,0:T(8,128)(2,1)} %get-tuple-element.501), channel_id=1, source_target_pairs={{0,2},{2,4},{4,6},{6,8},{8,10},{10,12},{12,14},{1,3},{3,5},{5,7},{... | collective-permute-start | bytes 294920 | tf_op jit(solution)/shard_map/while/body/eval_jaxpr/ppermute | solution.py:18
  321.2 59.4 %collective-permute-start.7 = (bf16[48,8,128]{2,1,0:T(8,128)(2,1)}, bf16[48,8,128]{2,1,0:T(8,128)(2,1)}, u32[]{:S(2)}, u32[]{:S(2)}) collective-permute-start(bf16[48,8,128]{2,1,0:T(8,128)(2,1)} %get-tuple-element.502), channel_id=1, source_target_pairs={{2,0},{4,2},{6,4},{8,6},{10,8},{12,10},{14,12},{3,1},{5,3},{7,5},{... | collective-permute-start | bytes 294920 | tf_op jit(solution)/shard_map/while/body/eval_jaxpr/ppermute | solution.py:20
  380.6 7.1 %copy-start = (f32[524288]{0:T(1024)S(1)}, f32[524288]{0:T(1024)}, u32[]{:S(2)}) copy-start(f32[524288]{0:T(1024)} %scatter_fusion) | copy-start | bytes 6291460 | tf_op jit(solution)/shard_map/while
  387.8 2.3 copy-start.5
  390.1 31.2 %copy-start.4 = (s32[1,3]{1,0:T(1,128)}, s32[1,3]{1,0:T(1,128)S(1)}, u32[]{:S(2)}) copy-start(s32[1,3]{1,0:T(1,128)S(1)} %get-tuple-element.548) | copy-start | bytes 40 | tf_op jit(solution)/shard_map/while
  391.1 19.7 %collective-permute-start = (f32[2,1,128,128]{3,2,1,0:T(8,128)S(1)}, f32[2,1,128,128]{3,2,1,0:T(8,128)S(1)}, u32[]{:S(2)}, u32[]{:S(2)}) collective-permute-start(f32[2,1,128,128]{3,2,1,0:T(8,128)S(1)} %get-tuple-element.488), channel_id=1, source_target_pairs={{0,16},{16,32},{32,48},{48,64},{64,80},{80,96},{96,112},{1,17},{17... | collective-permute-start | bytes 393224 | tf_op jit(solution)/shard_map/while/body/eval_jaxpr/ppermute | solution.py:18
  395.1 18.2 %collective-permute-start.1 = (f32[2,1,128,128]{3,2,1,0:T(8,128)S(1)}, f32[2,1,128,128]{3,2,1,0:T(8,128)S(1)}, u32[]{:S(2)}, u32[]{:S(2)}) collective-permute-start(f32[2,1,128,128]{3,2,1,0:T(8,128)S(1)} %get-tuple-element.489), channel_id=1, source_target_pairs={{16,0},{32,16},{48,32},{64,48},{80,64},{96,80},{112,96},{17,1},{33... | collective-permute-start | bytes 393224 | tf_op jit(solution)/shard_map/while/body/eval_jaxpr/ppermute | solution.py:20
  400.3 37.2 %collective-permute-start.4 = (bf16[8,128,128]{2,1,0:T(8,128)(2,1)}, bf16[8,128,128]{2,1,0:T(8,128)(2,1)S(1)}, u32[]{:S(2)}, u32[]{:S(2)}) collective-permute-start(bf16[8,128,128]{2,1,0:T(8,128)(2,1)} %get-tuple-element.499), channel_id=1, source_target_pairs={{16,0},{32,16},{48,32},{64,48},{80,64},{96,80},{112,96},{17,1},{33... | collective-permute-start | bytes 786440 | tf_op jit(solution)/shard_map/while/body/eval_jaxpr/ppermute | solution.py:20
  402.2 35.3 %collective-permute-start.5 = (bf16[8,128,128]{2,1,0:T(8,128)(2,1)}, bf16[8,128,128]{2,1,0:T(8,128)(2,1)}, u32[]{:S(2)}, u32[]{:S(2)}) collective-permute-start(bf16[8,128,128]{2,1,0:T(8,128)(2,1)} %get-tuple-element.500), channel_id=1, source_target_pairs={{0,16},{16,32},{32,48},{48,64},{64,80},{80,96},{96,112},{1,17},{17... | collective-permute-start | bytes 786440 | tf_op jit(solution)/shard_map/while/body/eval_jaxpr/ppermute | solution.py:18
  413.3 2.1 copy-start.2
  415.4 6.5 %collective-permute-start.2 = (f32[2,34,1,128]{3,2,1,0:T(1,128)S(1)}, f32[2,34,1,128]{3,2,1,0:T(1,128)S(1)}, u32[]{:S(2)}, u32[]{:S(2)}) collective-permute-start(f32[2,34,1,128]{3,2,1,0:T(1,128)S(1)} %get-tuple-element.490), channel_id=1, source_target_pairs={{2,0},{4,2},{6,4},{8,6},{10,8},{12,10},{14,12},{3,1},{5,3},{7,5},{... | collective-permute-start | bytes 104456 | tf_op jit(solution)/shard_map/while/body/eval_jaxpr/ppermute | solution.py:20
  417.3 7.9 %collective-permute-start.3 = (f32[2,34,1,128]{3,2,1,0:T(1,128)S(1)}, f32[2,34,1,128]{3,2,1,0:T(1,128)S(1)}, u32[]{:S(2)}, u32[]{:S(2)}) collective-permute-start(f32[2,34,1,128]{3,2,1,0:T(1,128)S(1)} %get-tuple-element.491), channel_id=1, source_target_pairs={{0,2},{2,4},{4,6},{6,8},{8,10},{10,12},{12,14},{1,3},{3,5},{5,7},{... | collective-permute-start | bytes 104456 | tf_op jit(solution)/shard_map/while/body/eval_jaxpr/ppermute | solution.py:18
  428.3 2.2 copy-start.1
  439.0 61.3 %collective-permute-start.6 = (bf16[48,8,128]{2,1,0:T(8,128)(2,1)}, bf16[48,8,128]{2,1,0:T(8,128)(2,1)S(1)}, u32[]{:S(2)}, u32[]{:S(2)}) collective-permute-start(bf16[48,8,128]{2,1,0:T(8,128)(2,1)} %get-tuple-element.501), channel_id=1, source_target_pairs={{0,2},{2,4},{4,6},{6,8},{8,10},{10,12},{12,14},{1,3},{3,5},{5,7},{... | collective-permute-start | bytes 294920 | tf_op jit(solution)/shard_map/while/body/eval_jaxpr/ppermute | solution.py:18
  440.9 59.4 %collective-permute-start.7 = (bf16[48,8,128]{2,1,0:T(8,128)(2,1)}, bf16[48,8,128]{2,1,0:T(8,128)(2,1)}, u32[]{:S(2)}, u32[]{:S(2)}) collective-permute-start(bf16[48,8,128]{2,1,0:T(8,128)(2,1)} %get-tuple-element.502), channel_id=1, source_target_pairs={{2,0},{4,2},{6,4},{8,6},{10,8},{12,10},{14,12},{3,1},{5,3},{7,5},{... | collective-permute-start | bytes 294920 | tf_op jit(solution)/shard_map/while/body/eval_jaxpr/ppermute | solution.py:20
  500.3 7.1 %copy-start = (f32[524288]{0:T(1024)S(1)}, f32[524288]{0:T(1024)}, u32[]{:S(2)}) copy-start(f32[524288]{0:T(1024)} %scatter_fusion) | copy-start | bytes 6291460 | tf_op jit(solution)/shard_map/while
  507.5 2.3 copy-start.5
Sparse Core Ops, SparseCore 0:
  9.7 18.7 all-gather.1
where the time goes:
time: 524 us; the launch traced here: 521 us
  other arithmetic  295 us (56%)
  starting transfers between devices  119 us (23%)
  local copies, waits for them, and re-layouts  63.9 us (12%)
  waiting for transfers between devices  26.5 us (5%)
  between operations  16.7 us (3%)
    scatter-add x4, other arithmetic, advance_step(): new_p = new_p.reshape(-1).at[target].add(amount, mode='drop').reshape(shape)  92.7 us
    scatter-add x4, other arithmetic, advance_step(): new_q = new_q.reshape(-1).at[target].add(amount, mode='drop').reshape(shape)  91.7 us
    ppermute x16, starting transfers between devices, with_halo(): lax.ppermute(tail, axis, [(i, (i + 1) % count) for i in range(ends)])  62.8 us
    ppermute x16, starting transfers between devices, with_halo(): lax.ppermute(head, axis, [((i + 1) % count, i) for i in range(ends)])  55.9 us
    while x52, local copies, waits for them, and re-layouts  33.5 us
    add x4, other arithmetic, advance(): new_p = 2.0 * p - old_p + horizontal + upright  28 us
    add x4, other arithmetic, advance_step(): image = image + jax.vmap(one_lag)(lag_offs)  27.9 us
    add x4, other arithmetic, advance(): new_q = 2.0 * q - old_q + ratio * horizontal + upright  21.3 us
  transfers between devices with their start and end apart: 33, of which 5 were waited for; matrix products, arithmetic and copies ran while one was open for 56% of the time, Pallas kernels for 0%

commit v1 on v0

v1 whole, which is shorter than its diff:
```python
import functools

import jax
import jax.numpy as jnp
from jax import lax
from jax.experimental import pallas as pl
from jax.experimental.pallas import tpu as pltpu
from jax.sharding import PartitionSpec as P

NT = 4
HMAX = 8
PAD = 8
CHUNK = 32
MESH = pl.DeviceIdType.MESH


def log2(n):
    bits = n.bit_length() - 1
    assert 1 << bits == n
    return bits


def inject_kernel(counts, pos_v, pos_s, data_s, out, link_v, link_s, sem):
    _, width_x, width_y, depth = out.shape
    rows = pos_v.shape[0]
    total = rows * 128
    bits_z, bits_y, bits_x = log2(depth), log2(width_y), log2(width_x)
    bits_gy = log2(counts[1])
    pos = pos_v[...]
    block_y = (pos >> (bits_z + bits_y)) & (counts[1] - 1)
    block_x = pos >> (bits_z + bits_y + bits_gy + bits_x)
    inside = (block_x == lax.axis_index("gx")) & (block_y == lax.axis_index("gy"))
    lane = lax.broadcasted_iota(jnp.int32, (rows, 128), 1)
    row = lax.broadcasted_iota(jnp.int32, (rows, 128), 0)
    link = jnp.where(inside, row * 128 + lane, total)
    step = 1
    while step < 128:
        ahead = pltpu.roll(link, 128 - step, 1)
        link = jnp.minimum(link, jnp.where(lane < 128 - step, ahead, total))
        step *= 2
    later = jnp.broadcast_to(link[:, :1], (rows, 128))
    later = jnp.where(row < rows - 1, pltpu.roll(later, rows - 1, 0), total)
    step = 1
    while step < rows:
        ahead = pltpu.roll(later, rows - step, 0)
        later = jnp.minimum(later, jnp.where(row < rows - step, ahead, total))
        step *= 2
    link_v[...] = jnp.minimum(link, later)
    copy = pltpu.make_async_copy(link_v, link_s, sem)
    copy.start()

    def clear(x, carry):
        for t in range(NT):
            out[t, x] = jnp.zeros((width_y, depth), jnp.float32)
        return carry

    lax.fori_loop(0, width_x, clear, 0)
    copy.wait()
    cell = lax.broadcasted_iota(jnp.int32, (1, depth), 1)

    def add(r):
        where = pos_s[r]
        x = (where >> (bits_z + bits_y + bits_gy)) & (width_x - 1)
        y = (where >> bits_z) & (width_y - 1)
        z = where & (depth - 1)
        hit = cell == z
        for t in range(NT):
            line = out[t, x, pl.ds(y, 1), :]
            out[t, x, pl.ds(y, 1), :] = line + jnp.where(hit, data_s[NT - 1 - t, r], 0.0)
        after = jnp.minimum(r + 1, total - 1)
        return jnp.where(r + 1 < total, link_s[after >> 7, after & 127], total)

    lax.while_loop(lambda r: r < total, add, link_s[0, 0])


def inject(counts, rec_pos, rec_data, shape):
    total = rec_pos.shape[0]
    rows = total // 128
    return pl.pallas_call(
        functools.partial(inject_kernel, counts),
        out_shape=jax.ShapeDtypeStruct((NT,) + shape, jnp.float32),
        in_specs=[
            pl.BlockSpec(memory_space=pltpu.VMEM),
            pl.BlockSpec(memory_space=pltpu.SMEM),
            pl.BlockSpec(memory_space=pltpu.SMEM),
        ],
        out_specs=pl.BlockSpec(memory_space=pltpu.VMEM),
        scratch_shapes=[
            pltpu.VMEM((rows, 128), jnp.int32),
            pltpu.SMEM((rows, 128), jnp.int32),
            pltpu.SemaphoreType.DMA,
        ],
        compiler_params=pltpu.CompilerParams(vmem_limit_bytes=20 << 20),
        name="inject",
    )(rec_pos.reshape(rows, 128), rec_pos, rec_data)


def march_kernel(
    counts,
    lag,
    src,
    rec_p,
    rec_q,
    prev_p,
    prev_q,
    horiz,
    vert,
    ratio,
    tilt,
    inj,
    image_out,
    p_out,
    q_out,
    f0, f1, f2, f3, f4,
    qa, qb,
    ch, cv, cr, ct,
    cinj,
    img,
    sx0, sx1, sx2, sx3,
    yl0, yl1, yl2, yl3,
    yr0, yr1, yr2, yr3,
    wide,
    xsend, xrecv, ysend, yrecv,
    load_sem,
    sx_sem, sy_sem, sc_sem, sm_sem,
    px_sem, py_sem,
    out_sem,
):
    n_gx, n_gy = counts
    gx, gy, mem = lax.axis_index("gx"), lax.axis_index("gy"), lax.axis_index("mem")
    width_x, width_y, depth = rec_p.shape
    last = width_x - 1
    sx = (sx0, sx1, sx2, sx3)
    yl = (yl0, yl1, yl2, yl3)
    yr = (yr0, yr1, yr2, yr3)
    own = pl.ds(HMAX, width_x)
    rows_in = pl.ds(PAD, width_y)

    loads = []

    def load(source, dest):
        copy = pltpu.make_async_copy(source, dest, load_sem.at[len(loads)])
        copy.start()
        loads.append(copy)

    load(rec_p, f0.at[:, rows_in])
    load(rec_q, qa)
    load(prev_p, f1.at[:, rows_in])
    load(horiz, ch)
    load(vert, cv)
    load(tilt, ct)
    load(prev_q, qb)
    load(ratio, cr)
    load(inj, cinj)
    load(src.at[0], sx0.at[own])
    load(src.at[1], sx1.at[own])

    def at(dgx, dgy):
        return ((gx + dgx + n_gx) % n_gx, (gy + dgy + n_gy) % n_gy, mem)

    peer = (gx, gy, 1 - mem)
    barrier = pltpu.get_barrier_semaphore()
    around = [(a, b) for a in (-1, 0, 1) for b in (-1, 0, 1) if (a, b) != (0, 0)]
    for a, b in around:
        pl.semaphore_signal(barrier, inc=1, device_id=at(a, b), device_id_type=MESH)
    pl.semaphore_signal(barrier, inc=1, device_id=peer, device_id_type=MESH)

    def exists(a, b):
        ok = True
        if a == -1:
            ok = gx > 0
        if a == 1:
            ok = gx < n_gx - 1
        if b == -1:
            ok_y = gy > 0
        if b == 1:
            ok_y = gy < n_gy - 1
        if b == 0:
            return ok
        if a == 0:
            return ok_y
        return ok & ok_y

    zero_row = jnp.zeros((1, depth), jnp.float32)

    def clear_pads(x, carry):
        for f in (f0, f1, f2, f3):
            f[x, PAD - 1 : PAD, :] = zero_row
            f[x, PAD + width_y : PAD + width_y + 1, :] = zero_row
        return carry

    lax.fori_loop(0, width_x, clear_pads, 0)

    spans = {-1: (0, HMAX), 0: (HMAX, width_x), 1: (HMAX + width_x, HMAX)}
    for j in range(2):
        for a in (-1, 1):
            first, n = spans[a]

            @pl.when(jnp.logical_not(exists(a, 0)))
            def _(j=j, first=first, n=n):
                for x in range(n):
                    sx[j][first + x] = jnp.zeros((width_y, depth), jnp.bfloat16)

        for b, side in ((-1, yl), (1, yr)):
            for a in (-1, 0, 1):
                first, n = spans[a]

                @pl.when(jnp.logical_not(exists(a, b)))
                def _(j=j, first=first, n=n, side=side):
                    def clear(x, carry):
                        side[j][first + x] = jnp.zeros((HMAX, depth), jnp.bfloat16)
                        return carry

                    lax.fori_loop(0, n, clear, 0)

    for a, side in ((-1, 0), (1, 1)):

        @pl.when(jnp.logical_not(exists(a, 0)))
        def _(side=side):
            for k in range(NT):
                for f in range(2):
                    xrecv[k, side, f] = jnp.zeros((width_y, depth), jnp.bfloat16)

        @pl.when(jnp.logical_not(exists(0, a)))
        def _(side=side):
            for k in range(NT):
                yrecv[k, side] = jnp.zeros((width_x, depth), jnp.float32)

    pl.semaphore_wait(barrier, len(around) + 1)

    def remote(source, dest, sems, i, target):
        return pltpu.make_async_remote_copy(
            src_ref=source,
            dst_ref=dest,
            send_sem=sems.at[0, i],
            recv_sem=sems.at[1, i],
            device_id=target,
            device_id_type=MESH,
        )

    def begin(a, b, copy):
        @pl.when(exists(a, b))
        def _():
            copy().start()

    def sent(a, b, copy):
        @pl.when(exists(a, b))
        def _():
            copy().wait_send()

    def landed(a, b, copy):
        @pl.when(exists(-a, -b))
        def _():
            copy().wait_recv()

    def edge(a, size):
        return pl.ds(size - HMAX, HMAX) if a == 1 else pl.ds(0, HMAX)

    def halo_x(a):
        first, n = spans[-a]
        return pl.ds(first, n)

    def source_x(j, a):
        i = j * 2 + (a + 1) // 2
        return lambda: remote(
            src.at[j, edge(a, width_x)], sx[j].at[halo_x(a)], sx_sem, i, at(a, 0)
        )

    def source_y(j, b):
        i = j * 2 + (b + 1) // 2
        dest = yl if b == 1 else yr
        return lambda: remote(
            src.at[j, :, edge(b, width_y)], dest[j].at[own], sy_sem, i, at(0, b)
        )

    def source_corner(j, a, b):
        i = j * 4 + (a + 1) + (b + 1) // 2
        dest = yl if b == 1 else yr
        return lambda: remote(
            src.at[j, edge(a, width_x), edge(b, width_y)],
            dest[j].at[halo_x(a)],
            sc_sem,
            i,
            at(a, b),
        )

    def to_peer(j, part):
        if part == 0:
            return remote(src.at[j], sx[2 + j].at[own], sm_sem, j, peer)
        if part == 1:
            here, there = sx[j].at[pl.ds(*spans[-1])], sx[2 + j].at[pl.ds(*spans[-1])]
        if part == 2:
            here, there = sx[j].at[pl.ds(*spans[1])], sx[2 + j].at[pl.ds(*spans[1])]
        if part == 3:
            here, there = yl[j], yl[2 + j]
        if part == 4:
            here, there = yr[j], yr[2 + j]
        return remote(here, there, sm_sem, part * 2 + j, peer)

    def field_x(k, a):
        side = (a + 1) // 2
        return lambda: remote(
            xsend.at[k, side], xrecv.at[k, 1 - side], px_sem, k * 2 + side, at(a, 0)
        )

    def field_y(k, b):
        side = (b + 1) // 2
        return lambda: remote(
            ysend.at[k, side], yrecv.at[k, 1 - side], py_sem, k * 2 + side, at(0, b)
        )

    fields = (f0, f1, f2, f3, f4)
    qs = (qa, qb)

    def stage_edges(k, p, q, rows):
        for side, x in ((0, 0), (1, last)):
            for y in range(0, width_y, CHUNK):
                xsend[k, side, 0, y : y + CHUNK, :] = p[
                    x, PAD + y : PAD + y + CHUNK, :
                ].astype(jnp.bfloat16)
                xsend[k, side, 1, y : y + CHUNK, :] = q[x, y : y + CHUNK, :].astype(
                    jnp.bfloat16
                )
        for a in (1, -1):
            begin(a, 0, field_x(k, a))
        if rows:

            def stage(x, carry):
                ysend[k, 0, pl.ds(x, 1), :] = p[x, PAD : PAD + 1, :]
                ysend[k, 1, pl.ds(x, 1), :] = p[x, PAD + width_y - 1 : PAD + width_y, :]
                return carry

            lax.fori_loop(0, width_x, stage, 0)
        for b in (1, -1):
            begin(0, b, field_y(k, b))

    lane = lax.broadcasted_iota(jnp.int32, (CHUNK, depth), 1)
    has_above = lane < depth - 1
    has_below = lane > 0

    def above(v):
        return jnp.where(has_above, pltpu.roll(v, depth - 1, 1), 0.0)

    def below(v):
        return jnp.where(has_below, pltpu.roll(v, 1, 1), 0.0)

    def plane(k, x, before, after):
        p, q = fields[k], qs[k % 2]
        old_p = fields[1] if k == 0 else fields[k - 1]
        new_p, new_q = fields[k + 1], qs[(k + 1) % 2]
        for y in range(0, width_y, CHUNK):
            own_rows = slice(y, y + CHUNK)
            pad_rows = slice(PAD + y, PAD + y + CHUNK)
            pc = p[x, pad_rows, :]
            lateral = (
                after(0, y)
                + before(0, y)
                + p[x, PAD + y + 1 : PAD + y + 1 + CHUNK, :]
                + p[x, PAD + y - 1 : PAD + y - 1 + CHUNK, :]
                - 4.0 * pc
            )
            qc = q[x, own_rows, :]
            slope = 0.25 * (after(1, y) - before(1, y))
            second = above(qc) + below(qc) - 2.0 * qc
            mixed = above(slope) - below(slope)
            added = cinj[k, x, own_rows, :]
            upright = cv[x, own_rows, :] * (second + ct[x, own_rows, :] * mixed) + added
            horizontal = ch[x, own_rows, :] * lateral
            new_p[x, pad_rows, :] = (2.0 * pc - old_p[x, pad_rows, :]) + horizontal + upright
            new_q[x, own_rows, :] = (
                (2.0 * qc - new_q[x, own_rows, :])
                + cr[x, own_rows, :] * horizontal
                + upright
            )

    def near(k, x):
        p, q = fields[k], qs[k % 2]

        def get(which, y):
            if which == 0:
                return p[x, PAD + y : PAD + y + CHUNK, :]
            return q[x, y : y + CHUNK, :]

        return get

    def far(k, side):
        def get(which, y):
            return xrecv[k, side, which, y : y + CHUNK, :].astype(jnp.float32)

        return get

    def mend(k):
        new_p, new_q = fields[k + 1], qs[(k + 1) % 2]

        def one(x, carry):
            for side, y in ((0, 0), (1, width_y - 1)):
                part = ch[x, y : y + 1, :] * yrecv[k, side, pl.ds(x, 1), :]
                line = new_p[x, PAD + y : PAD + y + 1, :] + part
                new_p[x, PAD + y : PAD + y + 1, :] = line
                if k < NT - 1:
                    ysend[k + 1, side, pl.ds(x, 1), :] = line
                new_q[x, y : y + 1, :] += cr[x, y : y + 1, :] * part
            return carry

        lax.fori_loop(0, width_x, one, 0, unroll=4)

    loads[0].wait()
    loads[1].wait()
    stage_edges(0, f0, qa, True)
    for j in range(2):
        to_peer(j, 0).start()
    for j in range(2):
        for a in (1, -1):
            for b in (1, -1):
                begin(a, b, source_corner(j, a, b))
        for b in (1, -1):
            begin(0, b, source_y(j, b))
    for copy in loads[2:]:
        copy.wait()

    for k in range(NT):
        j, a = k // 2, (1, -1)[k % 2]
        begin(a, 0, source_x(j, a))

        def inner(x, carry, k=k):
            plane(k, x, near(k, x - 1), near(k, x + 1))
            return carry

        lax.fori_loop(1, last, inner, 0)
        for side in (1, -1):
            landed(side, 0, field_x(k, side))
        plane(k, 0, far(k, 0), near(k, 1))
        plane(k, last, near(k, last - 1), far(k, 1))
        for side in (1, -1):
            landed(0, side, field_y(k, side))
        mend(k)
        if k < NT - 1:
            stage_edges(k + 1, fields[k + 1], qs[(k + 1) % 2], False)
        if k == 1:
            for j in range(2):
                for b in (1, -1):
                    landed(0, b, source_y(j, b))
                    for a in (1, -1):
                        landed(a, b, source_corner(j, a, b))
                for part in (3, 4):
                    to_peer(j, part).start()
        if k == 2:
            for a in (1, -1):
                landed(a, 0, source_x(0, a))
            for part in (1, 2):
                to_peer(0, part).start()

    outs = [
        pltpu.make_async_copy(f4.at[:, rows_in], p_out, out_sem.at[0]),
        pltpu.make_async_copy(qs[NT % 2], q_out, out_sem.at[1]),
    ]
    for copy in outs:
        copy.start()

    for a in (1, -1):
        landed(a, 0, source_x(1, a))
    for part in (1, 2):
        to_peer(1, part).start()
    for part in range(5):
        for j in range(2):
            to_peer(j, part).wait_recv()

    shift_x = lag[0, 0]
    shift_y = lag[0, 1]

    def times(s):
        return (2 * mem + s) if s < 2 else (2 * (1 - mem) + s - 2)

    def imaging(low):
        def by_plane(x, carry):
            at_x = x + HMAX - shift_x
            for s in range(4):
                wide[s, 0:HMAX, :] = yl[s][at_x].astype(jnp.float32)
                wide[s, HMAX : HMAX + width_y, :] = sx[s][at_x].astype(jnp.float32)
                wide[s, HMAX + width_y : 2 * HMAX + width_y, :] = yr[s][at_x].astype(
                    jnp.float32
                )
            for y in range(0, width_y, CHUNK):
                total = None
                for s in range(4):
                    k = NT - 1 - ((2 * low + s) if s < 2 else (2 * (1 - low) + s - 2))
                    piece = wide[s, pl.ds(HMAX - shift_y + y, CHUNK), :]
                    term = piece * fields[k][x, PAD + y : PAD + y + CHUNK, :]
                    total = term if total is None else total + term
                img[x, y : y + CHUNK, :] = total
            return carry

        lax.fori_loop(0, width_x, by_plane, 0)

    for m in range(2):

        @pl.when(mem == m)
        def _(m=m):
            imaging(m)

    outs.append(pltpu.make_async_copy(img, image_out.at[0], out_sem.at[2]))
    outs[-1].start()

    for k in range(NT):
        for a in (1, -1):
            sent(a, 0, field_x(k, a))
            sent(0, a, field_y(k, a))
    for j in range(2):
        for a in (1, -1):
            sent(a, 0, source_x(j, a))
            sent(0, a, source_y(j, a))
            for b in (1, -1):
                sent(a, b, source_corner(j, a, b))
        for part in range(5):
            to_peer(j, part).wait_send()
    for copy in outs:
        copy.wait()


def march(counts, lag, src, rec_p, rec_q, prev_p, prev_q, horiz, vert, ratio, tilt, inj):
    shape = rec_p.shape
    width_x, width_y, depth = shape
    padded = (width_x, width_y + 2 * PAD, depth)
    f32, bf16 = jnp.float32, jnp.bfloat16
    hbm = pl.BlockSpec(memory_space=pl.ANY)
    scratch = (
        [pltpu.VMEM(padded, f32)] * 5
        + [pltpu.VMEM(shape, f32)] * 2
        + [pltpu.VMEM(shape, f32)] * 4
        + [pltpu.VMEM((NT,) + shape, f32)]
        + [pltpu.VMEM(shape, f32)]
        + [pltpu.VMEM((width_x + 2 * HMAX, width_y, depth), bf16)] * 4
        + [pltpu.VMEM((width_x + 2 * HMAX, HMAX, depth), bf16)] * 8
        + [pltpu.VMEM((4, width_y + 2 * HMAX, depth), f32)]
        + [pltpu.VMEM((NT, 2, 2, width_y, depth), bf16)] * 2
        + [pltpu.VMEM((NT, 2, width_x, depth), f32)] * 2
        + [pltpu.SemaphoreType.DMA((11,))]
        + [pltpu.SemaphoreType.DMA((2, n)) for n in (4, 4, 8, 10, 2 * NT, 2 * NT)]
        + [pltpu.SemaphoreType.DMA((3,))]
    )
    return pl.pallas_call(
        functools.partial(march_kernel, counts),
        out_shape=(
            jax.ShapeDtypeStruct((1,) + shape, f32),
            jax.ShapeDtypeStruct(shape, f32),
            jax.ShapeDtypeStruct(shape, f32),
        ),
        in_specs=[pl.BlockSpec(memory_space=pltpu.SMEM)] + [hbm] * 10,
        out_specs=(hbm, hbm, hbm),
        scratch_shapes=scratch,
        compiler_params=pltpu.CompilerParams(
            collective_id=0, has_side_effects=True, vmem_limit_bytes=58 << 20
        ),
        name="march",
    )(lag, src, rec_p, rec_q, prev_p, prev_q, horiz, vert, ratio, tilt, inj)


def solution(mesh):
    counts = (mesh.shape["gx"], mesh.shape["gy"])

    def body(
        src_hist, rec_p, rec_q, prev_p, prev_q, horiz, vert, ratio, tilt, rec_pos, rec_data, lag_offs
    ):
        added = inject(counts, rec_pos, rec_data, rec_p.shape)
        return march(
            counts, lag_offs, src_hist, rec_p, rec_q, prev_p, prev_q, horiz, vert, ratio, tilt, added
        )

    cells = P("gx", "gy", None)
    return jax.shard_map(
        body,
        mesh=mesh,
        in_specs=(P("mem", "gx", "gy", None),) + (cells,) * 8 + (P(), P(), P("mem", None)),
        out_specs=(P("mem", "gx", "gy", None), cells, cells),
        check_vma=False,
    )
```

time: 524 us -> 84.1 us (0.16)
  the two profiles are of different devices: /device:TPU:6 before, /device:TPU:101 now
where the time goes in v1:
time: 84.1 us; the launch traced here: 83.9 us
  Pallas kernels  71.5 us (85%)
  local copies, waits for them, and re-layouts  11.7 us (14%)
    pallas_call x1, Pallas kernels, march(): pl.pallas_call(functools.partial(march_kernel, counts), out_shape=(jax.Sh...  67.3 us
    unnamed x13, local copies, waits for them, and re-layouts  11.7 us
    pallas_call x1, Pallas kernels, inject(): pl.pallas_call(functools.partial(inject_kernel, counts), out_shape=jax.Sh...  4.17 us

profile of v1, /device:TPU:101, one launch (start us, length us, event | category | flops | bytes accessed | tf_op | source)
XLA Modules:
  0.0 83.9 jit_solution(12934701738358480270)
XLA Ops:
  0.6 0.0 copy-start.1
  0.6 0.8 copy-done.1
  1.5 0.0 copy-start.2
  1.5 0.7 copy-done.2
  2.2 4.2 %inject.1.inj = f32[4,32,128,128]{3,2,1,0:T(8,128)S(1)} custom-call(s32[32,128]{1,0:T(8,128)S(1)} %bitcast.1, s32[4096]{0:T(1024)S(1)} %copy-done.2, f32[4,4096]{1,0:T(4,128)S(1)} %copy-done.1), custom_call_target="tpu_custom_call" | custom-call | tf_op jit(solution)/shard_map/inject/pallas_call | solution.py:79
  6.4 0.0 copy-start
  6.4 3.2 %copy-done = f32[4,32,128,128]{3,2,1,0:T(8,128)} copy-done((f32[4,32,128,128]{3,2,1,0:T(8,128)}, f32[4,32,128,128]{3,2,1,0:T(8,128)S(1)}, u32[]{:S(2)}) %copy-start) | copy-done | bytes 8388632
  9.6 67.3 %march.1 = (f32[1,32,128,128]{3,2,1,0:T(8,128)}, f32[32,128,128]{2,1,0:T(8,128)}, f32[32,128,128]{2,1,0:T(8,128)}) custom-call(s32[1,2]{1,0:T(1,128)} %lag.1, bf16[2,32,128,128]{3,2,1,0:T(8,128)(2,1)} %src.1, f32[32,128,128]{2,1,0:T(8,128)} %rec_p.1, f32[32,128,128]{2,1,0:T(8,128)} %rec_q.1, f32[32,128,128]{2,1,0:T(8,128)} %prev_p.1, ...), custom_call_target="tpu_custom_call" | custom-call | tf_op jit(solution)/shard_map/march/pallas_call | solution.py:541
  76.9 0.0 copy-start.4
  76.9 3.3 %copy.18 = f32[1,32,128,128]{3,2,1,0:T(8,128)} copy(f32[1,32,128,128]{3,2,1,0:T(8,128)} %get-tuple-element.6) | data formatting | bytes 4194304
  80.2 0.0 copy-done.4
  80.2 0.0 copy-start.3
  80.2 1.3 %copy.19 = f32[32,128,128]{2,1,0:T(8,128)} copy(f32[32,128,128]{2,1,0:T(8,128)S(1)} %copy-done.4) | data formatting | bytes 4194304
  81.5 1.0 %copy-done.3 = f32[32,128,128]{2,1,0:T(8,128)S(1)} copy-done((f32[32,128,128]{2,1,0:T(8,128)S(1)}, f32[32,128,128]{2,1,0:T(8,128)}, u32[]{:S(2)}) %copy-start.3) | copy-done | bytes 2097176
  82.6 1.3 %copy.20 = f32[32,128,128]{2,1,0:T(8,128)} copy(f32[32,128,128]{2,1,0:T(8,128)S(1)} %copy-done.3) | data formatting | bytes 4194304
Async XLA Ops:
  0.6 0.8 %copy-start.1 = (f32[4,4096]{1,0:T(4,128)S(1)}, f32[4,4096]{1,0:T(4,128)}, u32[]{:S(2)}) copy-start(f32[4,4096]{1,0:T(4,128)} %data_s.1) | copy-start | bytes 196612
  1.5 0.7 copy-start.2
  6.4 3.2 %copy-start = (f32[4,32,128,128]{3,2,1,0:T(8,128)}, f32[4,32,128,128]{3,2,1,0:T(8,128)S(1)}, u32[]{:S(2)}) copy-start(f32[4,32,128,128]{3,2,1,0:T(8,128)S(1)} %inject.1.inj) | copy-start | bytes 25165828
  76.9 3.3 %copy-start.4 = (f32[32,128,128]{2,1,0:T(8,128)S(1)}, f32[32,128,128]{2,1,0:T(8,128)}, u32[]{:S(2)}) copy-start(f32[32,128,128]{2,1,0:T(8,128)} %get-tuple-element.7) | copy-start | bytes 6291460
  80.2 2.3 %copy-start.3 = (f32[32,128,128]{2,1,0:T(8,128)S(1)}, f32[32,128,128]{2,1,0:T(8,128)}, u32[]{:S(2)}) copy-start(f32[32,128,128]{2,1,0:T(8,128)} %get-tuple-element.8) | copy-start | bytes 6291460

commit v2 on v1

--- a/solution.py
+++ b/solution.py
@@ -10,6 +10,8 @@
 NT = 4
 HMAX = 8
 PAD = 8
+PIECE = 4
+REACHES = (0, 4, 8)
 CHUNK = 32
 MESH = pl.DeviceIdType.MESH
 
@@ -20,15 +22,31 @@
     return bits
 
 
-def inject_kernel(counts, pos_v, pos_s, data_s, out, link_v, link_s, sem):
+def inject_kernel(
+    counts, pos_rows, pos, data, out, pos_v, pos_s, data_s, link_v, link_s, sem
+):
     _, width_x, width_y, depth = out.shape
+    staged = [
+        pltpu.make_async_copy(here, there, sem.at[i])
+        for i, (here, there) in enumerate(((pos_rows, pos_v), (pos, pos_s), (data, data_s)))
+    ]
+    for copy in staged:
+        copy.start()
+
+    def clear(x, carry):
+        for t in range(NT):
+            out[t, x] = jnp.zeros((width_y, depth), jnp.float32)
+        return carry
+
+    lax.fori_loop(0, width_x // 2, clear, 0)
     rows = pos_v.shape[0]
     total = rows * 128
     bits_z, bits_y, bits_x = log2(depth), log2(width_y), log2(width_x)
     bits_gy = log2(counts[1])
-    pos = pos_v[...]
-    block_y = (pos >> (bits_z + bits_y)) & (counts[1] - 1)
-    block_x = pos >> (bits_z + bits_y + bits_gy + bits_x)
+    staged[0].wait()
+    place = pos_v[...]
+    block_y = (place >> (bits_z + bits_y)) & (counts[1] - 1)
+    block_x = place >> (bits_z + bits_y + bits_gy + bits_x)
     inside = (block_x == lax.axis_index("gx")) & (block_y == lax.axis_index("gy"))
     lane = lax.broadcasted_iota(jnp.int32, (rows, 128), 1)
     row = lax.broadcasted_iota(jnp.int32, (rows, 128), 0)
@@ -46,16 +64,12 @@
         later = jnp.minimum(later, jnp.where(row < rows - step, ahead, total))
         step *= 2
     link_v[...] = jnp.minimum(link, later)
-    copy = pltpu.make_async_copy(link_v, link_s, sem)
+    copy = pltpu.make_async_copy(link_v, link_s, sem.at[3])
     copy.start()
-
-    def clear(x, carry):
-        for t in range(NT):
-            out[t, x] = jnp.zeros((width_y, depth), jnp.float32)
-        return carry
-
-    lax.fori_loop(0, width_x, clear, 0)
+    lax.fori_loop(width_x // 2, width_x, clear, 0)
     copy.wait()
+    for copy in staged[1:]:
+        copy.wait()
     cell = lax.broadcasted_iota(jnp.int32, (1, depth), 1)
 
     def add(r):
@@ -79,24 +93,29 @@
     return pl.pallas_call(
         functools.partial(inject_kernel, counts),
         out_shape=jax.ShapeDtypeStruct((NT,) + shape, jnp.float32),
-        in_specs=[
-            pl.BlockSpec(memory_space=pltpu.VMEM),
-            pl.BlockSpec(memory_space=pltpu.SMEM),
-            pl.BlockSpec(memory_space=pltpu.SMEM),
-        ],
+        in_specs=[pl.BlockSpec(memory_space=pltpu.HBM)] * 3,
         out_specs=pl.BlockSpec(memory_space=pltpu.VMEM),
         scratch_shapes=[
             pltpu.VMEM((rows, 128), jnp.int32),
+            pltpu.SMEM((total,), jnp.int32),
+            pltpu.SMEM(rec_data.shape, jnp.float32),
+            pltpu.VMEM((rows, 128), jnp.int32),
             pltpu.SMEM((rows, 128), jnp.int32),
-            pltpu.SemaphoreType.DMA,
+            pltpu.SemaphoreType.DMA((4,)),
         ],
         compiler_params=pltpu.CompilerParams(vmem_limit_bytes=20 << 20),
         name="inject",
-    )(rec_pos.reshape(rows, 128), rec_pos, rec_data)
+    )(
+        *(
+            pltpu.with_memory_space_constraint(v, pltpu.HBM)
+            for v in (rec_pos.reshape(rows, 128), rec_pos, rec_data)
+        )
+    )
 
 
 def march_kernel(
     counts,
+    reach,
     lag,
     src,
     rec_p,
@@ -111,11 +130,9 @@
     image_out,
     p_out,
     q_out,
-    f0, f1, f2, f3, f4,
+    f0, f1, f2, f3,
     qa, qb,
     ch, cv, cr, ct,
-    cinj,
-    img,
     sx0, sx1, sx2, sx3,
     yl0, yl1, yl2, yl3,
     yr0, yr1, yr2, yr3,
@@ -124,7 +141,6 @@
     load_sem,
     sx_sem, sy_sem, sc_sem, sm_sem,
     px_sem, py_sem,
-    out_sem,
 ):
     n_gx, n_gy = counts
     gx, gy, mem = lax.axis_index("gx"), lax.axis_index("gy"), lax.axis_index("mem")
@@ -151,7 +167,6 @@
     load(tilt, ct)
     load(prev_q, qb)
     load(ratio, cr)
-    load(inj, cinj)
     load(src.at[0], sx0.at[own])
     load(src.at[1], sx1.at[own])
 
@@ -191,7 +206,8 @@
 
     lax.fori_loop(0, width_x, clear_pads, 0)
 
-    spans = {-1: (0, HMAX), 0: (HMAX, width_x), 1: (HMAX + width_x, HMAX)}
+    spans = {-1: (0, HMAX), 0: (HMAX, width_x), 1: (HMAX + width_x, reach)}
+    sides = (1, -1) if reach else (1,)
     for j in range(2):
         for a in (-1, 1):
             first, n = spans[a]
@@ -204,6 +220,8 @@
         for b, side in ((-1, yl), (1, yr)):
             for a in (-1, 0, 1):
                 first, n = spans[a]
+                if not n:
+                    continue
 
                 @pl.when(jnp.logical_not(exists(a, b)))
                 def _(j=j, first=first, n=n, side=side):
@@ -225,8 +243,6 @@
         def _(side=side):
             for k in range(NT):
                 yrecv[k, side] = jnp.zeros((width_x, depth), jnp.float32)
-
-    pl.semaphore_wait(barrier, len(around) + 1)
 
     def remote(source, dest, sems, i, target):
         return pltpu.make_async_remote_copy(
@@ -253,31 +269,46 @@
         def _():
             copy().wait_recv()
 
-    def edge(a, size):
-        return pl.ds(size - HMAX, HMAX) if a == 1 else pl.ds(0, HMAX)
+    def edge_x(a):
+        return pl.ds(width_x - HMAX, HMAX) if a == 1 else pl.ds(0, reach)
+
+    def edge_y(b):
+        return pl.ds(width_y - HMAX, HMAX) if b == 1 else pl.ds(0, HMAX)
 
     def halo_x(a):
         first, n = spans[-a]
         return pl.ds(first, n)
 
-    def source_x(j, a):
-        i = j * 2 + (a + 1) // 2
+    def source_x(j, a, part):
+        i = j * 4 + (a + 1) + part
+        first = width_x - HMAX if a == 1 else 0
         return lambda: remote(
-            src.at[j, edge(a, width_x)], sx[j].at[halo_x(a)], sx_sem, i, at(a, 0)
-        )
+            src.at[j, pl.ds(first + part * PIECE, PIECE)],
+            sx[j].at[pl.ds(spans[-a][0] + part * PIECE, PIECE)],
+            sx_sem,
+            i,
+            at(a, 0),
+        )
+
+    halves = (1, 2) if reach else (1,)
+    parts = (0,) + halves + (3, 4)
+    pieces = [
+        [(j, a, part) for part in range(2) for a in sides if part * PIECE < spans[-a][1]]
+        for j in range(2)
+    ]
 
     def source_y(j, b):
         i = j * 2 + (b + 1) // 2
         dest = yl if b == 1 else yr
         return lambda: remote(
-            src.at[j, :, edge(b, width_y)], dest[j].at[own], sy_sem, i, at(0, b)
+            src.at[j, :, edge_y(b)], dest[j].at[own], sy_sem, i, at(0, b)
         )
 
     def source_corner(j, a, b):
         i = j * 4 + (a + 1) + (b + 1) // 2
         dest = yl if b == 1 else yr
         return lambda: remote(
-            src.at[j, edge(a, width_x), edge(b, width_y)],
+            src.at[j, edge_x(a), edge_y(b)],
             dest[j].at[halo_x(a)],
             sc_sem,
             i,
@@ -291,10 +322,11 @@
             here, there = sx[j].at[pl.ds(*spans[-1])], sx[2 + j].at[pl.ds(*spans[-1])]
         if part == 2:
             here, there = sx[j].at[pl.ds(*spans[1])], sx[2 + j].at[pl.ds(*spans[1])]
+        used = pl.ds(0, HMAX + width_x + reach)
         if part == 3:
-            here, there = yl[j], yl[2 + j]
+            here, there = yl[j].at[used], yl[2 + j].at[used]
         if part == 4:
-            here, there = yr[j], yr[2 + j]
+            here, there = yr[j].at[used], yr[2 + j].at[used]
         return remote(here, there, sm_sem, part * 2 + j, peer)
 
     def field_x(k, a):
@@ -309,10 +341,12 @@
             ysend.at[k, side], yrecv.at[k, 1 - side], py_sem, k * 2 + side, at(0, b)
         )
 
-    fields = (f0, f1, f2, f3, f4)
-    qs = (qa, qb)
-
-    def stage_edges(k, p, q, rows):
+    fields = (f0, f1, f2, f3, p_out)
+    qs = (qa, qb, qa, qb, q_out)
+    pads = (PAD, PAD, PAD, PAD, 0)
+
+    def stage_planes(k):
+        p, q = fields[k], qs[k]
         for side, x in ((0, 0), (1, last)):
             for y in range(0, width_y, CHUNK):
                 xsend[k, side, 0, y : y + CHUNK, :] = p[
@@ -321,18 +355,30 @@
                 xsend[k, side, 1, y : y + CHUNK, :] = q[x, y : y + CHUNK, :].astype(
                     jnp.bfloat16
                 )
+
+    def send_planes(k):
         for a in (1, -1):
             begin(a, 0, field_x(k, a))
-        if rows:
-
-            def stage(x, carry):
-                ysend[k, 0, pl.ds(x, 1), :] = p[x, PAD : PAD + 1, :]
-                ysend[k, 1, pl.ds(x, 1), :] = p[x, PAD + width_y - 1 : PAD + width_y, :]
-                return carry
-
-            lax.fori_loop(0, width_x, stage, 0)
+
+    def stage_rows(k):
+        p = fields[k]
+
+        def stage(x, carry):
+            ysend[k, 0, pl.ds(x, 1), :] = p[x, PAD : PAD + 1, :]
+            ysend[k, 1, pl.ds(x, 1), :] = p[x, PAD + width_y - 1 : PAD + width_y, :]
+            return carry
+
+        lax.fori_loop(0, width_x, stage, 0, unroll=4)
+
+    def send_rows(k):
         for b in (1, -1):
             begin(0, b, field_y(k, b))
+
+    loads[0].wait()
+    loads[1].wait()
+    stage_planes(0)
+    stage_rows(0)
+    pl.semaphore_wait(barrier, len(around) + 1)
 
     lane = lax.broadcasted_iota(jnp.int32, (CHUNK, depth), 1)
     has_above = lane < depth - 1
@@ -345,9 +391,10 @@
         return jnp.where(has_below, pltpu.roll(v, 1, 1), 0.0)
 
     def plane(k, x, before, after):
-        p, q = fields[k], qs[k % 2]
-        old_p = fields[1] if k == 0 else fields[k - 1]
-        new_p, new_q = fields[k + 1], qs[(k + 1) % 2]
+        p, q = fields[k], qs[k]
+        old_p, old_q = (fields[1], qs[1]) if k == 0 else (fields[k - 1], qs[k - 1])
+        new_p, new_q = fields[k + 1], qs[k + 1]
+        pad = pads[k + 1]
         for y in range(0, width_y, CHUNK):
             own_rows = slice(y, y + CHUNK)
             pad_rows = slice(PAD + y, PAD + y + CHUNK)
@@ -363,18 +410,18 @@
             slope = 0.25 * (after(1, y) - before(1, y))
             second = above(qc) + below(qc) - 2.0 * qc
             mixed = above(slope) - below(slope)
-            added = cinj[k, x, own_rows, :]
+            added = inj[k, x, own_rows, :]
             upright = cv[x, own_rows, :] * (second + ct[x, own_rows, :] * mixed) + added
             horizontal = ch[x, own_rows, :] * lateral
-            new_p[x, pad_rows, :] = (2.0 * pc - old_p[x, pad_rows, :]) + horizontal + upright
+            new_p[x, pad + y : pad + y + CHUNK, :] = (2.0 * pc - old_p[x, pad_rows, :]) + horizontal + upright
             new_q[x, own_rows, :] = (
-                (2.0 * qc - new_q[x, own_rows, :])
+                (2.0 * qc - old_q[x, own_rows, :])
                 + cr[x, own_rows, :] * horizontal
                 + upright
             )
 
     def near(k, x):
-        p, q = fields[k], qs[k % 2]
+        p, q = fields[k], qs[k]
 
         def get(which, y):
             if which == 0:
@@ -390,27 +437,33 @@
         return get
 
     def mend(k):
-        new_p, new_q = fields[k + 1], qs[(k + 1) % 2]
+        new_p, new_q, pad = fields[k + 1], qs[k + 1], pads[k + 1]
 
         def one(x, carry):
             for side, y in ((0, 0), (1, width_y - 1)):
                 part = ch[x, y : y + 1, :] * yrecv[k, side, pl.ds(x, 1), :]
-                line = new_p[x, PAD + y : PAD + y + 1, :] + part
-                new_p[x, PAD + y : PAD + y + 1, :] = line
+                line = new_p[x, pad + y : pad + y + 1, :] + part
+                new_p[x, pad + y : pad + y + 1, :] = line
                 if k < NT - 1:
                     ysend[k + 1, side, pl.ds(x, 1), :] = line
                 new_q[x, y : y + 1, :] += cr[x, y : y + 1, :] * part
             return carry
 
-        lax.fori_loop(0, width_x, one, 0, unroll=4)
-
-    loads[0].wait()
-    loads[1].wait()
-    stage_edges(0, f0, qa, True)
+        for x in (0, last):
+            one(x, 0)
+        if k < NT - 1:
+            stage_planes(k + 1)
+            send_planes(k + 1)
+        lax.fori_loop(1, last, one, 0, unroll=3)
+        if k < NT - 1:
+            send_rows(k + 1)
+
+    send_planes(0)
+    send_rows(0)
     for j in range(2):
         to_peer(j, 0).start()
     for j in range(2):
-        for a in (1, -1):
+        for a in sides:
             for b in (1, -1):
                 begin(a, b, source_corner(j, a, b))
         for b in (1, -1):
@@ -419,8 +472,10 @@
         copy.wait()
 
     for k in range(NT):
-        j, a = k // 2, (1, -1)[k % 2]
-        begin(a, 0, source_x(j, a))
+        mine = pieces[k // 2]
+        half = (len(mine) + 1) // 2
+        for j, a, part in mine[half:] if k % 2 else mine[:half]:
+            begin(a, 0, source_x(j, a, part))
 
         def inner(x, carry, k=k):
             plane(k, x, near(k, x - 1), near(k, x + 1))
@@ -434,34 +489,23 @@
         for side in (1, -1):
             landed(0, side, field_y(k, side))
         mend(k)
-        if k < NT - 1:
-            stage_edges(k + 1, fields[k + 1], qs[(k + 1) % 2], False)
-        if k == 1:
-            for j in range(2):
-                for b in (1, -1):
-                    landed(0, b, source_y(j, b))
-                    for a in (1, -1):
-                        landed(a, b, source_corner(j, a, b))
-                for part in (3, 4):
-                    to_peer(j, part).start()
-        if k == 2:
-            for a in (1, -1):
-                landed(a, 0, source_x(0, a))
-            for part in (1, 2):
-                to_peer(0, part).start()
-
-    outs = [
-        pltpu.make_async_copy(f4.at[:, rows_in], p_out, out_sem.at[0]),
-        pltpu.make_async_copy(qs[NT % 2], q_out, out_sem.at[1]),
-    ]
-    for copy in outs:
-        copy.start()
-
-    for a in (1, -1):
-        landed(a, 0, source_x(1, a))
-    for part in (1, 2):
+
+    for j, a, part in pieces[0]:
+        landed(a, 0, source_x(j, a, part))
+    for part in halves:
+        to_peer(0, part).start()
+    for j in range(2):
+        for b in (1, -1):
+            landed(0, b, source_y(j, b))
+            for a in sides:
+                landed(a, b, source_corner(j, a, b))
+        for part in (3, 4):
+            to_peer(j, part).start()
+    for j, a, part in pieces[1]:
+        landed(a, 0, source_x(j, a, part))
+    for part in halves:
         to_peer(1, part).start()
-    for part in range(5):
+    for part in parts:
         for j in range(2):
             to_peer(j, part).wait_recv()
 
@@ -487,7 +531,7 @@
                     piece = wide[s, pl.ds(HMAX - shift_y + y, CHUNK), :]
                     term = piece * fields[k][x, PAD + y : PAD + y + CHUNK, :]
                     total = term if total is None else total + term
-                img[x, y : y + CHUNK, :] = total
+                image_out[0, x, y : y + CHUNK, :] = total
             return carry
 
         lax.fori_loop(0, width_x, by_plane, 0)
@@ -497,62 +541,80 @@
         @pl.when(mem == m)
         def _(m=m):
             imaging(m)
-
-    outs.append(pltpu.make_async_copy(img, image_out.at[0], out_sem.at[2]))
-    outs[-1].start()
 
     for k in range(NT):
         for a in (1, -1):
             sent(a, 0, field_x(k, a))
             sent(0, a, field_y(k, a))
     for j in range(2):
-        for a in (1, -1):
-            sent(a, 0, source_x(j, a))
-            sent(0, a, source_y(j, a))
-            for b in (1, -1):
+        for piece in pieces[j]:
+            sent(piece[1], 0, source_x(*piece))
+        for b in (1, -1):
+            sent(0, b, source_y(j, b))
+            for a in sides:
                 sent(a, b, source_corner(j, a, b))
-        for part in range(5):
+        for part in parts:
             to_peer(j, part).wait_send()
-    for copy in outs:
+
+
+def land_kernel(*refs):
+    sem = refs[-1]
+    count = len(refs) // 2
+    copies = [
+        pltpu.make_async_copy(refs[i], refs[count + i], sem.at[i]) for i in range(count)
+    ]
+    for copy in copies:
+        copy.start()
+    for copy in copies:
         copy.wait()
 
 
-def march(counts, lag, src, rec_p, rec_q, prev_p, prev_q, horiz, vert, ratio, tilt, inj):
+def land(*results):
+    return pl.pallas_call(
+        land_kernel,
+        out_shape=tuple(jax.ShapeDtypeStruct(r.shape, r.dtype) for r in results),
+        in_specs=[pl.BlockSpec(memory_space=pl.ANY)] * len(results),
+        out_specs=tuple(pl.BlockSpec(memory_space=pltpu.HBM) for r in results),
+        scratch_shapes=[pltpu.SemaphoreType.DMA((len(results),))],
+        compiler_params=pltpu.CompilerParams(vmem_limit_bytes=1 << 20),
+        name="land",
+    )(*results)
+
+
+def march(counts, reach, lag, src, rec_p, rec_q, prev_p, prev_q, horiz, vert, ratio, tilt, inj):
     shape = rec_p.shape
     width_x, width_y, depth = shape
     padded = (width_x, width_y + 2 * PAD, depth)
     f32, bf16 = jnp.float32, jnp.bfloat16
-    hbm = pl.BlockSpec(memory_space=pl.ANY)
+    hbm = pl.BlockSpec(memory_space=pltpu.HBM)
+    vmem = pl.BlockSpec(memory_space=pltpu.VMEM)
     scratch = (
-        [pltpu.VMEM(padded, f32)] * 5
+        [pltpu.VMEM(padded, f32)] * 4
         + [pltpu.VMEM(shape, f32)] * 2
         + [pltpu.VMEM(shape, f32)] * 4
-        + [pltpu.VMEM((NT,) + shape, f32)]
-        + [pltpu.VMEM(shape, f32)]
         + [pltpu.VMEM((width_x + 2 * HMAX, width_y, depth), bf16)] * 4
         + [pltpu.VMEM((width_x + 2 * HMAX, HMAX, depth), bf16)] * 8
         + [pltpu.VMEM((4, width_y + 2 * HMAX, depth), f32)]
         + [pltpu.VMEM((NT, 2, 2, width_y, depth), bf16)] * 2
         + [pltpu.VMEM((NT, 2, width_x, depth), f32)] * 2
-        + [pltpu.SemaphoreType.DMA((11,))]
-        + [pltpu.SemaphoreType.DMA((2, n)) for n in (4, 4, 8, 10, 2 * NT, 2 * NT)]
-        + [pltpu.SemaphoreType.DMA((3,))]
+        + [pltpu.SemaphoreType.DMA((10,))]
+        + [pltpu.SemaphoreType.DMA((2, n)) for n in (8, 4, 8, 10, 2 * NT, 2 * NT)]
     )
-    return pl.pallas_call(
-        functools.partial(march_kernel, counts),
+    return land(*pl.pallas_call(
+        functools.partial(march_kernel, counts, reach),
         out_shape=(
             jax.ShapeDtypeStruct((1,) + shape, f32),
             jax.ShapeDtypeStruct(shape, f32),
             jax.ShapeDtypeStruct(shape, f32),
         ),
-        in_specs=[pl.BlockSpec(memory_space=pltpu.SMEM)] + [hbm] * 10,
-        out_specs=(hbm, hbm, hbm),
+        in_specs=[pl.BlockSpec(memory_space=pltpu.SMEM)] + [hbm] * 9 + [vmem],
+        out_specs=(vmem, vmem, vmem),
         scratch_shapes=scratch,
         compiler_params=pltpu.CompilerParams(
-            collective_id=0, has_side_effects=True, vmem_limit_bytes=58 << 20
+            collective_id=REACHES.index(reach), has_side_effects=True, vmem_limit_bytes=38 << 20
         ),
-        name="march",
-    )(lag, src, rec_p, rec_q, prev_p, prev_q, horiz, vert, ratio, tilt, inj)
+        name=f"march{reach}",
+    )(lag, src, rec_p, rec_q, prev_p, prev_q, horiz, vert, ratio, tilt, inj))
 
 
 def solution(mesh):
@@ -562,8 +624,13 @@
         src_hist, rec_p, rec_q, prev_p, prev_q, horiz, vert, ratio, tilt, rec_pos, rec_data, lag_offs
     ):
         added = inject(counts, rec_pos, rec_data, rec_p.shape)
-        return march(
-            counts, lag_offs, src_hist, rec_p, rec_q, prev_p, prev_q, horiz, vert, ratio, tilt, added
+        other = lax.ppermute(lag_offs, "mem", [(0, 1), (1, 0)])
+        need = -jnp.minimum(lag_offs[0, 0], other[0, 0])
+        branch = sum((need > r).astype(jnp.int32) for r in REACHES[:-1])
+        return lax.switch(
+            branch,
+            [functools.partial(march, counts, r) for r in REACHES],
+            lag_offs, src_hist, rec_p, rec_q, prev_p, prev_q, horiz, vert, ratio, tilt, added,
         )
 
     cells = P("gx", "gy", None)

time: 84.1 us -> 48.3 us (0.57)
  the two profiles are of different devices: /device:TPU:101 before, /device:TPU:27 now
where the time goes in v2:
time: 48.3 us; the launch traced here: 48.1 us
  Pallas kernels  46.6 us (96%)
  starting transfers between devices  0.75 us (2%)
  between operations  0.75 us (2%)
    pallas_call x1, Pallas kernels, march(): pl.pallas_call(functools.partial(march_kernel, counts, reach), out_shape=...  40.5 us
    pallas_call x1, Pallas kernels, inject(): pl.pallas_call(functools.partial(inject_kernel, counts), out_shape=jax.Sh...  3.39 us
    pallas_call x1, Pallas kernels, land(): pl.pallas_call(land_kernel, out_shape=tuple((jax.ShapeDtypeStruct(r.shape...  2.73 us
  transfers between devices with their start and end apart: 1, of which 0 were waited for; matrix products, arithmetic and copies ran while one was open for 0% of the time, Pallas kernels for 7%

profile of v2, /device:TPU:27, one launch (start us, length us, event | category | flops | bytes accessed | tf_op | source)
XLA Modules:
  0.0 48.1 jit_solution(9972024602808587836)
XLA Ops:
  0.6 0.8 %collective-permute-start = (s32[1,2]{1,0:T(1,128)}, s32[1,2]{1,0:T(1,128)S(1)}, u32[]{:S(2)}, u32[]{:S(2)}) collective-permute-start(s32[1,2]{1,0:T(1,128)} %param.26), channel_id=1, source_target_pairs={{0,1},{1,0},{2,3},{3,2},{4,5},{5,4},{6,7},{7,6},{8,9},{9,8},{10,11... | collective-permute-start | bytes 32 | tf_op jit(solution)/shard_map/ppermute | solution.py:627
  1.4 0.0 copy-start.4
  1.4 0.0 copy-start
  1.4 0.0 copy-start.1
  1.4 0.0 copy-start.2
  1.4 0.0 copy-start.3
  1.4 3.4 %inject.1 = f32[4,32,128,128]{3,2,1,0:T(8,128)S(1)} custom-call(s32[32,128]{1,0:T(8,128)} %bitcast.4, s32[4096]{0:T(1024)} %pos.1, f32[4,4096]{1,0:T(4,128)} %data.1), custom_call_target="tpu_custom_call" | custom-call | tf_op jit(solution)/shard_map/inject/pallas_call | solution.py:93
  4.8 0.0 collective-permute-done
  4.8 0.0 copy-done.4
  4.9 0.0 copy-done
  4.9 0.0 copy-done.1
  4.9 0.0 copy-done.2
  4.9 0.0 copy-done.3
  4.9 43.2 %conditional.1 = ((f32[1,32,128,128]{3,2,1,0:T(8,128)}, f32[32,128,128]{2,1,0:T(8,128)}, f32[32,128,128]{2,1,0:T(8,128)})) conditional(s32[]{:T(128)} %bitcast, (s32[1,2]{1,0:T(1,128)S(1)}, bf16[2,32,128,128]{3,2,1,0:T(8,128)(2,1)S(1)}, f32[32,128,128]{2,1,0:T(8,128)S(1)}, f32[32,128,128]{2,1,0:T(8,128)S(1)}, ...), branch_computations={%region_0.0_spmd, %region_1.0_spmd, %region_2.0_spmd} | conditional | bytes 8 | solution.py:630
  4.9 40.5 %march0.1 = (f32[1,32,128,128]{3,2,1,0:T(8,128)S(1)}, f32[32,128,128]{2,1,0:T(8,128)S(1)}, f32[32,128,128]{2,1,0:T(8,128)S(1)}) custom-call(s32[1,2]{1,0:T(1,128)S(1)} %get-tuple-element.66.lag, bf16[2,32,128,128]{3,2,1,0:T(8,128)(2,1)S(1)} %get-tuple-element.67.src, f32[32,128,128]{2,1,0:T(8,128)S(1)} %get-tuple-element.68.rec_p, ...), custom_call_target="tpu_custom_call" | custom-call | tf_op jit(solution)/shard_map/cond/branch_0_fun/march0/pallas_call | solution.py:603
  45.4 2.7 %land.3 = (f32[1,32,128,128]{3,2,1,0:T(8,128)}, f32[32,128,128]{2,1,0:T(8,128)}, f32[32,128,128]{2,1,0:T(8,128)}) custom-call(f32[1,32,128,128]{3,2,1,0:T(8,128)S(1)} %get-tuple-element.77.refs_0_, f32[32,128,128]{2,1,0:T(8,128)S(1)} %get-tuple-element.78.refs_1_, f32[32,128,128]{2,1,0:T(8,128)S(1)} %get-tuple-element.79.refs_2_), custom_call_target="tpu_custom_call" | custom-call | tf_op jit(solution)/shard_map/cond/branch_0_fun/land/pallas_call | solution.py:573
Async XLA Ops:
  0.6 4.2 %collective-permute-start = (s32[1,2]{1,0:T(1,128)}, s32[1,2]{1,0:T(1,128)S(1)}, u32[]{:S(2)}, u32[]{:S(2)}) collective-permute-start(s32[1,2]{1,0:T(1,128)} %param.26), channel_id=1, source_target_pairs={{0,1},{1,0},{2,3},{3,2},{4,5},{5,4},{6,7},{7,6},{8,9},{9,8},{10,11... | collective-permute-start | bytes 32 | tf_op jit(solution)/shard_map/ppermute | solution.py:627
  1.4 3.4 %copy-start.4 = (s32[1,2]{1,0:T(1,128)S(1)}, s32[1,2]{1,0:T(1,128)}, u32[]{:S(2)}) copy-start(s32[1,2]{1,0:T(1,128)} %param.26) | copy-start | bytes 28
  1.4 3.5 %copy-start = (bf16[2,32,128,128]{3,2,1,0:T(8,128)(2,1)S(1)}, bf16[2,32,128,128]{3,2,1,0:T(8,128)(2,1)}, u32[]{:S(2)}) copy-start(bf16[2,32,128,128]{3,2,1,0:T(8,128)(2,1)} %param.15) | copy-start | bytes 6291460
  1.4 3.5 %copy-start.1 = (f32[32,128,128]{2,1,0:T(8,128)S(1)}, f32[32,128,128]{2,1,0:T(8,128)}, u32[]{:S(2)}) copy-start(f32[32,128,128]{2,1,0:T(8,128)} %param.16) | copy-start | bytes 6291460
  1.4 3.5 %copy-start.2 = (f32[32,128,128]{2,1,0:T(8,128)S(1)}, f32[32,128,128]{2,1,0:T(8,128)}, u32[]{:S(2)}) copy-start(f32[32,128,128]{2,1,0:T(8,128)} %param.17) | copy-start | bytes 6291460
  1.4 3.5 %copy-start.3 = (f32[32,128,128]{2,1,0:T(8,128)S(1)}, f32[32,128,128]{2,1,0:T(8,128)}, u32[]{:S(2)}) copy-start(f32[32,128,128]{2,1,0:T(8,128)} %param.18) | copy-start | bytes 6291460

commit v3 on v2

--- a/solution.py
+++ b/solution.py
@@ -11,7 +11,7 @@
 HMAX = 8
 PAD = 8
 PIECE = 4
-REACHES = (0, 4, 8)
+REACHES = (0, 2, 4, 6, 8)
 CHUNK = 32
 MESH = pl.DeviceIdType.MESH
 
@@ -140,7 +140,7 @@
     xsend, xrecv, ysend, yrecv,
     load_sem,
     sx_sem, sy_sem, sc_sem, sm_sem,
-    px_sem, py_sem,
+    px_sem, py_sem, pm_sem,
 ):
     n_gx, n_gy = counts
     gx, gy, mem = lax.axis_index("gx"), lax.axis_index("gy"), lax.axis_index("mem")
@@ -282,9 +282,10 @@
     def source_x(j, a, part):
         i = j * 4 + (a + 1) + part
         first = width_x - HMAX if a == 1 else 0
+        size = min(PIECE, spans[-a][1] - part * PIECE)
         return lambda: remote(
-            src.at[j, pl.ds(first + part * PIECE, PIECE)],
-            sx[j].at[pl.ds(spans[-a][0] + part * PIECE, PIECE)],
+            src.at[j, pl.ds(first + part * PIECE, size)],
+            sx[j].at[pl.ds(spans[-a][0] + part * PIECE, size)],
             sx_sem,
             i,
             at(a, 0),
@@ -332,8 +333,13 @@
     def field_x(k, a):
         side = (a + 1) // 2
         return lambda: remote(
-            xsend.at[k, side], xrecv.at[k, 1 - side], px_sem, k * 2 + side, at(a, 0)
-        )
+            xsend.at[k, side], xrecv.at[k, 1 - side, mem], px_sem, k * 2 + side, at(a, 0)
+        )
+
+    def shared_x(k, a):
+        side = (a + 1) // 2
+        here = xrecv.at[k, 1 - side, mem]
+        return lambda: remote(here, here, pm_sem, k * 2 + side, peer)
 
     def field_y(k, b):
         side = (b + 1) // 2
@@ -348,13 +354,14 @@
     def stage_planes(k):
         p, q = fields[k], qs[k]
         for side, x in ((0, 0), (1, last)):
-            for y in range(0, width_y, CHUNK):
-                xsend[k, side, 0, y : y + CHUNK, :] = p[
-                    x, PAD + y : PAD + y + CHUNK, :
-                ].astype(jnp.bfloat16)
-                xsend[k, side, 1, y : y + CHUNK, :] = q[x, y : y + CHUNK, :].astype(
-                    jnp.bfloat16
-                )
+
+            @pl.when(mem == 0)
+            def _(side=side, x=x):
+                xsend[k, side] = p[x, PAD : PAD + width_y, :].astype(jnp.bfloat16)
+
+            @pl.when(mem == 1)
+            def _(side=side, x=x):
+                xsend[k, side] = q[x].astype(jnp.bfloat16)
 
     def send_planes(k):
         for a in (1, -1):
@@ -471,80 +478,93 @@
     for copy in loads[2:]:
         copy.wait()
 
-    for k in range(NT):
-        mine = pieces[k // 2]
-        half = (len(mine) + 1) // 2
-        for j, a, part in mine[half:] if k % 2 else mine[:half]:
-            begin(a, 0, source_x(j, a, part))
-
-        def inner(x, carry, k=k):
-            plane(k, x, near(k, x - 1), near(k, x + 1))
+    def imaging(low, slots, fresh):
+        def by_plane(x, carry):
+            at_x = x + HMAX - lag[0, 0]
+            for s in slots:
+                wide[s, 0:HMAX, :] = yl[s][at_x].astype(jnp.float32)
+                wide[s, HMAX : HMAX + width_y, :] = sx[s][at_x].astype(jnp.float32)
+                wide[s, HMAX + width_y : 2 * HMAX + width_y, :] = yr[s][at_x].astype(
+                    jnp.float32
+                )
+            for y in range(0, width_y, CHUNK):
+                total = None if fresh else image_out[0, x, y : y + CHUNK, :]
+                for s in slots:
+                    k = NT - 1 - ((2 * low + s) if s < 2 else (2 * (1 - low) + s - 2))
+                    piece = wide[s, pl.ds(HMAX - lag[0, 1] + y, CHUNK), :]
+                    term = piece * fields[k][x, PAD + y : PAD + y + CHUNK, :]
+                    total = term if total is None else total + term
+                image_out[0, x, y : y + CHUNK, :] = total
             return carry
 
-        lax.fori_loop(1, last, inner, 0)
-        for side in (1, -1):
-            landed(side, 0, field_x(k, side))
-        plane(k, 0, far(k, 0), near(k, 1))
-        plane(k, last, near(k, last - 1), far(k, 1))
-        for side in (1, -1):
-            landed(0, side, field_y(k, side))
-        mend(k)
-
-    for j, a, part in pieces[0]:
-        landed(a, 0, source_x(j, a, part))
-    for part in halves:
-        to_peer(0, part).start()
-    for j in range(2):
+        lax.fori_loop(0, width_x, by_plane, 0)
+
+    def image_slots(slots, fresh):
+        for m in range(2):
+
+            @pl.when(mem == m)
+            def _(m=m):
+                imaging(m, slots, fresh)
+
+    def forward(j):
+        for piece in pieces[j]:
+            landed(piece[1], 0, source_x(*piece))
+        for part in halves:
+            to_peer(j, part).start()
         for b in (1, -1):
             landed(0, b, source_y(j, b))
             for a in sides:
                 landed(a, b, source_corner(j, a, b))
         for part in (3, 4):
             to_peer(j, part).start()
-    for j, a, part in pieces[1]:
-        landed(a, 0, source_x(j, a, part))
-    for part in halves:
-        to_peer(1, part).start()
-    for part in parts:
-        for j in range(2):
+
+    def collect(j):
+        for part in parts:
             to_peer(j, part).wait_recv()
 
-    shift_x = lag[0, 0]
-    shift_y = lag[0, 1]
-
-    def times(s):
-        return (2 * mem + s) if s < 2 else (2 * (1 - mem) + s - 2)
-
-    def imaging(low):
-        def by_plane(x, carry):
-            at_x = x + HMAX - shift_x
-            for s in range(4):
-                wide[s, 0:HMAX, :] = yl[s][at_x].astype(jnp.float32)
-                wide[s, HMAX : HMAX + width_y, :] = sx[s][at_x].astype(jnp.float32)
-                wide[s, HMAX + width_y : 2 * HMAX + width_y, :] = yr[s][at_x].astype(
-                    jnp.float32
-                )
-            for y in range(0, width_y, CHUNK):
-                total = None
-                for s in range(4):
-                    k = NT - 1 - ((2 * low + s) if s < 2 else (2 * (1 - low) + s - 2))
-                    piece = wide[s, pl.ds(HMAX - shift_y + y, CHUNK), :]
-                    term = piece * fields[k][x, PAD + y : PAD + y + CHUNK, :]
-                    total = term if total is None else total + term
-                image_out[0, x, y : y + CHUNK, :] = total
+    early = reach == 0
+    for k in range(NT):
+        mine = pieces[k // 2]
+        half = (len(mine) + 1) // 2
+        for j, a, part in mine[half:] if k % 2 else mine[:half]:
+            begin(a, 0, source_x(j, a, part))
+
+        def inner(x, carry, k=k):
+            plane(k, x, near(k, x - 1), near(k, x + 1))
             return carry
 
-        lax.fori_loop(0, width_x, by_plane, 0)
-
-    for m in range(2):
-
-        @pl.when(mem == m)
-        def _(m=m):
-            imaging(m)
+        lax.fori_loop(1, last, inner, 0)
+        if early and k == NT - 1:
+            collect(0)
+            image_slots((0, 2), True)
+        for side in (1, -1):
+            landed(side, 0, field_x(k, side))
+            begin(-side, 0, shared_x(k, side))
+        for side in (1, -1):
+            landed(side, 0, shared_x(k, side))
+        plane(k, 0, far(k, 0), near(k, 1))
+        plane(k, last, near(k, last - 1), far(k, 1))
+        for side in (1, -1):
+            landed(0, side, field_y(k, side))
+        mend(k)
+        if early and k == NT - 2:
+            forward(0)
+
+    if early:
+        forward(1)
+        collect(1)
+        image_slots((1, 3), False)
+    else:
+        forward(0)
+        forward(1)
+        collect(0)
+        collect(1)
+        image_slots((0, 1, 2, 3), True)
 
     for k in range(NT):
         for a in (1, -1):
             sent(a, 0, field_x(k, a))
+            sent(-a, 0, shared_x(k, a))
             sent(0, a, field_y(k, a))
     for j in range(2):
         for piece in pieces[j]:
@@ -595,10 +615,10 @@
         + [pltpu.VMEM((width_x + 2 * HMAX, width_y, depth), bf16)] * 4
         + [pltpu.VMEM((width_x + 2 * HMAX, HMAX, depth), bf16)] * 8
         + [pltpu.VMEM((4, width_y + 2 * HMAX, depth), f32)]
-        + [pltpu.VMEM((NT, 2, 2, width_y, depth), bf16)] * 2
+        + [pltpu.VMEM((NT, 2, width_y, depth), bf16), pltpu.VMEM((NT, 2, 2, width_y, depth), bf16)]
         + [pltpu.VMEM((NT, 2, width_x, depth), f32)] * 2
         + [pltpu.SemaphoreType.DMA((10,))]
-        + [pltpu.SemaphoreType.DMA((2, n)) for n in (8, 4, 8, 10, 2 * NT, 2 * NT)]
+        + [pltpu.SemaphoreType.DMA((2, n)) for n in (8, 4, 8, 10, 2 * NT, 2 * NT, 2 * NT)]
     )
     return land(*pl.pallas_call(
         functools.partial(march_kernel, counts, reach),

time: 48.3 us -> 47.1 us (0.975)
  the two profiles are of different devices: /device:TPU:27 before, /device:TPU:1 now
where the time goes in v3:
time: 47.1 us; the launch traced here: 46.9 us
  Pallas kernels  44.6 us (95%)
  starting transfers between devices  1.5 us (3%)
  between operations  0.74 us (2%)
    pallas_call x1, Pallas kernels, march(): pl.pallas_call(functools.partial(march_kernel, counts, reach), out_shape=...  38.6 us
    pallas_call x1, Pallas kernels, inject(): pl.pallas_call(functools.partial(inject_kernel, counts), out_shape=jax.Sh...  3.28 us
    pallas_call x1, Pallas kernels, land(): pl.pallas_call(land_kernel, out_shape=tuple((jax.ShapeDtypeStruct(r.shape...  2.73 us
    ppermute x1, starting transfers between devices, body(): other = lax.ppermute(lag_offs, 'mem', [(0, 1), (1, 0)])  1.5 us
  transfers between devices with their start and end apart: 1, of which 0 were waited for; matrix products, arithmetic and copies ran while one was open for 0% of the time, Pallas kernels for 7%

profile of v3, /device:TPU:1, one launch (start us, length us, event | category | flops | bytes accessed | tf_op | source)
XLA Modules:
  0.0 46.9 jit_solution(8549740665680593450)
XLA Ops:
  0.6 1.5 %collective-permute-start = (s32[1,2]{1,0:T(1,128)}, s32[1,2]{1,0:T(1,128)S(1)}, u32[]{:S(2)}, u32[]{:S(2)}) collective-permute-start(s32[1,2]{1,0:T(1,128)} %param.28), channel_id=1, source_target_pairs={{0,1},{1,0},{2,3},{3,2},{4,5},{5,4},{6,7},{7,6},{8,9},{9,8},{10,11... | collective-permute-start | bytes 32 | tf_op jit(solution)/shard_map/ppermute | solution.py:647
  2.1 0.0 copy-start.4
  2.1 0.0 copy-start
  2.1 0.0 copy-start.1
  2.1 0.0 copy-start.2
  2.1 0.0 copy-start.3
  2.2 3.3 %inject.1 = f32[4,32,128,128]{3,2,1,0:T(8,128)S(1)} custom-call(s32[32,128]{1,0:T(8,128)} %bitcast.4, s32[4096]{0:T(1024)} %pos.1, f32[4,4096]{1,0:T(4,128)} %data.1), custom_call_target="tpu_custom_call" | custom-call | tf_op jit(solution)/shard_map/inject/pallas_call | solution.py:93
  5.4 0.0 collective-permute-done
  5.5 0.0 copy-done.4
  5.5 0.0 copy-done
  5.5 0.0 copy-done.1
  5.5 0.0 copy-done.2
  5.5 0.1 copy-done.3
  5.6 41.3 %conditional.1 = ((f32[1,32,128,128]{3,2,1,0:T(8,128)}, f32[32,128,128]{2,1,0:T(8,128)}, f32[32,128,128]{2,1,0:T(8,128)})) conditional(s32[]{:T(128)} %bitcast, (s32[1,2]{1,0:T(1,128)S(1)}, bf16[2,32,128,128]{3,2,1,0:T(8,128)(2,1)S(1)}, f32[32,128,128]{2,1,0:T(8,128)S(1)}, f32[32,128,128]{2,1,0:T(8,128)S(1)}, ...), branch_computations={%region_0.0_spmd, %region_1.0_spmd, %region_2.0_spmd, %region_3.0_... | conditional | bytes 8 | solution.py:650
  5.6 38.6 %march0.1 = (f32[1,32,128,128]{3,2,1,0:T(8,128)S(1)}, f32[32,128,128]{2,1,0:T(8,128)S(1)}, f32[32,128,128]{2,1,0:T(8,128)S(1)}) custom-call(s32[1,2]{1,0:T(1,128)S(1)} %get-tuple-element.110.lag, bf16[2,32,128,128]{3,2,1,0:T(8,128)(2,1)S(1)} %get-tuple-element.111.src, f32[32,128,128]{2,1,0:T(8,128)S(1)} %get-tuple-element.112.rec_p, ...), custom_call_target="tpu_custom_call" | custom-call | tf_op jit(solution)/shard_map/cond/branch_0_fun/march0/pallas_call | solution.py:623
  44.2 2.7 %land.5 = (f32[1,32,128,128]{3,2,1,0:T(8,128)}, f32[32,128,128]{2,1,0:T(8,128)}, f32[32,128,128]{2,1,0:T(8,128)}) custom-call(f32[1,32,128,128]{3,2,1,0:T(8,128)S(1)} %get-tuple-element.121.refs_0_, f32[32,128,128]{2,1,0:T(8,128)S(1)} %get-tuple-element.122.refs_1_, f32[32,128,128]{2,1,0:T(8,128)S(1)} %get-tuple-element.123.refs_2_), custom_call_target="tpu_custom_call" | custom-call | tf_op jit(solution)/shard_map/cond/branch_0_fun/land/pallas_call | solution.py:593
Async XLA Ops:
  0.6 4.8 %collective-permute-start = (s32[1,2]{1,0:T(1,128)}, s32[1,2]{1,0:T(1,128)S(1)}, u32[]{:S(2)}, u32[]{:S(2)}) collective-permute-start(s32[1,2]{1,0:T(1,128)} %param.28), channel_id=1, source_target_pairs={{0,1},{1,0},{2,3},{3,2},{4,5},{5,4},{6,7},{7,6},{8,9},{9,8},{10,11... | collective-permute-start | bytes 32 | tf_op jit(solution)/shard_map/ppermute | solution.py:647
  2.1 3.3 %copy-start.4 = (s32[1,2]{1,0:T(1,128)S(1)}, s32[1,2]{1,0:T(1,128)}, u32[]{:S(2)}) copy-start(s32[1,2]{1,0:T(1,128)} %param.28) | copy-start | bytes 28
  2.1 3.4 %copy-start = (bf16[2,32,128,128]{3,2,1,0:T(8,128)(2,1)S(1)}, bf16[2,32,128,128]{3,2,1,0:T(8,128)(2,1)}, u32[]{:S(2)}) copy-start(bf16[2,32,128,128]{3,2,1,0:T(8,128)(2,1)} %param.17) | copy-start | bytes 6291460
  2.1 3.4 %copy-start.1 = (f32[32,128,128]{2,1,0:T(8,128)S(1)}, f32[32,128,128]{2,1,0:T(8,128)}, u32[]{:S(2)}) copy-start(f32[32,128,128]{2,1,0:T(8,128)} %param.18) | copy-start | bytes 6291460
  2.1 3.4 %copy-start.2 = (f32[32,128,128]{2,1,0:T(8,128)S(1)}, f32[32,128,128]{2,1,0:T(8,128)}, u32[]{:S(2)}) copy-start(f32[32,128,128]{2,1,0:T(8,128)} %param.19) | copy-start | bytes 6291460
  2.1 3.5 %copy-start.3 = (f32[32,128,128]{2,1,0:T(8,128)S(1)}, f32[32,128,128]{2,1,0:T(8,128)}, u32[]{:S(2)}) copy-start(f32[32,128,128]{2,1,0:T(8,128)} %param.20) | copy-start | bytes 6291460
